TPU v7x, 256 devices: a whole 4x4x8 slice. The times are simulated.
256 devices in a mesh: vel: 16 (over z, core), cx: 4 (over y), cy: 4 (over x).
Axes of the slice: x: 4, y: 4, z: 8, core: 2. Of those that a mesh axis runs over, the one named last changes fastest.
Arguments:
- distribution: float32 [64, 16, 4, 13824], P('cx', 'cy', None, 'vel'), may hold values from 0.1 to 2
- refine_level: int32 [64, 16, 4], P('cx', 'cy'), may hold values from 0 to 2, as said below
- gain_one: float32 [24, 24, 24], replicated, may hold values from 0 to 2
- gain_two: float32 [24, 24, 24], replicated, may hold values from 0 to 2
- loss_kernel: float32 [24, 24, 24], replicated, may hold values from 0 to 2
Outputs:
- evolved: float32 [64, 16, 4, 13824], P('cx', 'cy', None, 'vel')
Inputs may be any that keep to these rules, and one draw needn't show every extreme that they name: `refine_level`: in each block of 256 cells (the 16 x 4 x 4 cells of one index of cx and cy) at most 128 cells have a level above 0, and some block has exactly 128.
All inputs are finite; a program needn't handle non-finite values.
Results may differ from a plain program's by a relative error of at most 0.0022.
Values may be sent and summed in bfloat16 or wider, within the bound.
A program may use at most 64 MiB of HBM per device.

v0:
```python
import math

import jax
import jax.numpy as jnp
from jax import lax
from jax.sharding import Mesh
from jax.sharding import PartitionSpec as P

VEL = ("vel_0", "vel_1")


def extended(array, sides, width):
    edges = {}
    for axis, dim in sides:
        count, length = (lax.axis_size(axis), array.shape[dim])
        up = [(i, (i + 1) % count) for i in range(count)]
        last = lax.slice_in_dim(array, length - width, length, axis=dim)
        leading = lax.slice_in_dim(array, 0, width, axis=dim)
        edges[dim] = (
            lax.ppermute(last, axis, up),
            lax.ppermute(leading, axis, [(b, a) for a, b in up]),
        )
    done = []
    for _, dim in sides:
        low, high = edges[dim]
        around = [(width, width) if d in done else (0, 0) for d in range(array.ndim)]
        array = jnp.concatenate([jnp.pad(low, around), array, jnp.pad(high, around)], axis=dim)
        done.append(dim)
    return array


def cut_along(array, dim, count):
    shape = array.shape
    parts = array.reshape(*shape[:dim], count, shape[dim] // count, *shape[dim + 1 :])
    return jnp.moveaxis(parts, dim, 0)


def laid_out(parts, dim):
    parts = jnp.moveaxis(parts, 0, dim)
    shape = parts.shape
    return parts.reshape(*shape[:dim], shape[dim] * shape[dim + 1], *shape[dim + 2 :])


def turned_blocks(parts, axes, turns):
    inside = parts.shape[1:]
    out = parts.reshape(*(lax.axis_size(a) for a in axes), *inside)
    for k in turns:
        out = lax.all_to_all(out, axes[k], k, k, tiled=True)
    return out.reshape(-1, *inside)


def exchange_by_axis(array, axes, turns, split_dim, concat_dim):
    parts = cut_along(array, split_dim, lax.axis_size(axes))
    return laid_out(turned_blocks(parts, axes, turns), concat_dim)


def dft_tables(points):
    indices = jnp.arange(points, dtype=jnp.int32)
    products = indices[:, None] * indices[None, :] % points
    angles = products.astype(jnp.float32) * (2.0 * math.pi / points)
    cosine = jnp.cos(angles)
    sine_table = jnp.sin(angles)
    forward = jnp.stack([jnp.stack([cosine, sine_table]), jnp.stack([-sine_table, cosine])])
    inverse = jnp.stack([jnp.stack([cosine, -sine_table]), jnp.stack([sine_table, cosine])])
    return (forward.astype(jnp.bfloat16), inverse.astype(jnp.bfloat16))


def contract(pattern, left_side, right_side):
    return jnp.einsum(pattern, left_side, right_side, preferred_element_type=jnp.float32)


def collide(cells, forward, inverse, gain_one, gain_two, loss_kernel):
    points = forward.shape[-1]
    cell_count = cells.shape[0]
    field = cells.reshape(cell_count, points, points, points)
    section_z = contract("nabz,qzw->qnabw", field, forward[:, 0]).astype(jnp.bfloat16)
    section_y = contract("pnayc,qpyw->qnawc", section_z, forward).astype(jnp.bfloat16)
    spectrum = contract("pnxbc,qpxw->qnwbc", section_y, forward)
    scale_factor = 1.0 / float(points**3)

    def filtered(kernel):
        weighted = (spectrum * (kernel * scale_factor)[None, None]).astype(jnp.bfloat16)
        back_x = contract("pnxbc,qpxw->qnwbc", weighted, inverse).astype(jnp.bfloat16)
        back_y = contract("pnayc,qpyw->qnawc", back_x, inverse).astype(jnp.bfloat16)
        return contract("pnabz,pzw->nabw", back_y, inverse[0])

    gain_term = filtered(gain_one) * filtered(gain_two)
    result = gain_term - field.astype(jnp.float32) * filtered(loss_kernel)
    return result.reshape(cell_count, points**3)


def courants(points, first_vel, local_count):
    vel_index = first_vel + jnp.arange(local_count, dtype=jnp.int32)
    index_x = vel_index // (points * points)
    index_y = vel_index // points % points
    index_z = vel_index % points

    def speed(index_part):
        return 0.3 * (2.0 * index_part.astype(jnp.float32) - (points - 1)) / (points - 1)

    return (speed(index_x), speed(index_y), speed(index_z))


def upwind_flux(courant, center, lower_side, upper_side):
    return jnp.maximum(courant, 0.0) * (center - lower_side) + jnp.minimum(courant, 0.0) * (
        upper_side - center
    )


def per_device(distribution, refine_level, gain_one, gain_two, loss_kernel):
    points = gain_one.shape[0]
    width_x, width_y, width_z, local_vel = distribution.shape
    first_vel = lax.axis_index(VEL) * local_vel
    courant_x, courant_y, courant_z = courants(points, first_vel, local_vel)
    padded = extended(distribution, (("cx", 0), ("cy", 1)), 1)
    fluxes = upwind_flux(courant_x, distribution, padded[:-2, 1:-1], padded[2:, 1:-1])
    fluxes = fluxes + upwind_flux(courant_y, distribution, padded[1:-1, :-2], padded[1:-1, 2:])
    fluxes = fluxes + upwind_flux(
        courant_z, distribution, jnp.roll(distribution, 1, 2), jnp.roll(distribution, -1, 2)
    )
    read = distribution - fluxes
    block_cells = width_x * width_y * width_z
    groups = lax.axis_size(VEL)
    flattened = read.reshape(block_cells, local_vel).astype(jnp.bfloat16)
    forward, inverse = dft_tables(points)
    active = refine_level.reshape(block_cells) > 0
    slot_index = jnp.cumsum(active.astype(jnp.int32)) - 1
    capacity = block_cells // 2
    picker = (
        (slot_index[None, :] == jnp.arange(capacity, dtype=jnp.int32)[:, None]) & active[None, :]
    ).astype(jnp.bfloat16)
    chosen = jnp.dot(picker, flattened, preferred_element_type=jnp.float32).astype(jnp.bfloat16)
    terms = collide(
        lax.all_to_all(
            chosen.reshape(groups, capacity // groups, local_vel),
            VEL,
            split_axis=0,
            concat_axis=2,
            tiled=True,
        )[0],
        forward,
        inverse,
        gain_one,
        gain_two,
        loss_kernel,
    )[None]
    packed = exchange_by_axis(terms.astype(jnp.bfloat16), VEL, (1, 0), 2, 0).astype(terms.dtype)
    packed_rows = packed.reshape(capacity, local_vel)
    safe_slot = jnp.clip(slot_index, 0, capacity - 1)
    rates = jnp.where(active[:, None], packed_rows[safe_slot], 0.0)
    weight = 0.25 * refine_level.astype(jnp.float32)
    return read + weight[..., None] * rates.reshape(width_x, width_y, width_z, local_vel)


def solution(mesh):
    torus = Mesh(
        mesh.devices.reshape(8, 2, mesh.shape["cx"], mesh.shape["cy"]),
        ("vel_0", "vel_1", "cx", "cy"),
    )
    in_specs = (P("cx", "cy", None, VEL), P("cx", "cy", None), P(), P(), P())
    out_specs = P("cx", "cy", None, VEL)
    return jax.shard_map(
        per_device, mesh=torus, in_specs=in_specs, out_specs=out_specs, check_vma=False
    )
```

profile of v0, /device:TPU:1, one launch (start us, length us, event | category | flops | bytes accessed | tf_op | source)
XLA Modules:
  0.0 95.7 jit_solution(18153332531370563100)
XLA Ops:
  0.0 1.6 %fusion.141 = (f32[1,4,4,864]{3,2,1,0:T(4,128)}, f32[1,4,4,864]{3,2,1,0:T(4,128)}) fusion(f32[16,4,4,864]{3,2,1,0:T(4,128)} %param.5), kind=kLoop, calls=%fused_computation.171 | loop fusion | bytes 221184 | tf_op jit(solution)/shard_map/slice | solution.py:18
  1.6 2.1 %collective-permute-start = (f32[1,4,4,864]{3,2,1,0:T(4,128)}, f32[1,4,4,864]{3,2,1,0:T(4,128)S(1)}, u32[]{:S(2)}, u32[]{:S(2)}) collective-permute-start(f32[1,4,4,864]{3,2,1,0:T(4,128)} %get-tuple-element.15), channel_id=1, source_target_pairs={{0,4},{4,8},{8,12},{12,0},{1,5},{5,9},{9,13},{13,1},{2,6},{6,10},{... | collective-permute-start | bytes 165896 | tf_op jit(solution)/shard_map/ppermute | solution.py:20
  3.7 1.4 %collective-permute-start.1 = (f32[1,4,4,864]{3,2,1,0:T(4,128)}, f32[1,4,4,864]{3,2,1,0:T(4,128)S(1)}, u32[]{:S(2)}, u32[]{:S(2)}) collective-permute-start(f32[1,4,4,864]{3,2,1,0:T(4,128)} %get-tuple-element.14), channel_id=1, source_target_pairs={{4,0},{8,4},{12,8},{0,12},{5,1},{9,5},{13,9},{1,13},{6,2},{10,6},{... | collective-permute-start | bytes 165896 | tf_op jit(solution)/shard_map/ppermute | solution.py:21
  5.1 1.9 %fusion.140 = (f32[16,1,4,864]{3,2,1,0:T(4,128)}, f32[16,1,4,864]{3,2,1,0:T(4,128)}) fusion(f32[16,4,4,864]{3,2,1,0:T(4,128)} %param.5), kind=kLoop, calls=%fused_computation.170 | loop fusion | bytes 884736 | tf_op jit(solution)/shard_map/slice | solution.py:17
  7.0 1.2 %collective-permute-start.2 = (f32[16,1,4,864]{3,2,1,0:T(4,128)}, f32[16,1,4,864]{3,2,1,0:T(4,128)}, u32[]{:S(2)}, u32[]{:S(2)}) collective-permute-start(f32[16,1,4,864]{3,2,1,0:T(4,128)} %get-tuple-element.12), channel_id=1, source_target_pairs={{0,1},{1,2},{2,3},{3,0},{4,5},{5,6},{6,7},{7,4},{8,9},{9,10},{10,1... | collective-permute-start | bytes 663560 | tf_op jit(solution)/shard_map/ppermute | solution.py:20
  8.2 1.5 %collective-permute-start.3 = (f32[16,1,4,864]{3,2,1,0:T(4,128)}, f32[16,1,4,864]{3,2,1,0:T(4,128)}, u32[]{:S(2)}, u32[]{:S(2)}) collective-permute-start(f32[16,1,4,864]{3,2,1,0:T(4,128)} %get-tuple-element.13), channel_id=1, source_target_pairs={{1,0},{2,1},{3,2},{0,3},{5,4},{6,5},{7,6},{4,7},{9,8},{10,9},{11,1... | collective-permute-start | bytes 663560 | tf_op jit(solution)/shard_map/ppermute | solution.py:21
  10.1 1.1 %fusion.142 = (f32[16,4,1,864]{3,2,1,0:T(1,128)}, f32[16,4,1,864]{3,2,1,0:T(1,128)}) fusion(f32[16,4,4,864]{3,2,1,0:T(4,128)S(1)} %copy-done), kind=kLoop, calls=%fused_computation.172 | loop fusion | bytes 884736 | tf_op jit(solution)/shard_map/jit(_roll_static)/slice | solution.py:119
  14.9 5.0 %fusion.138 = (bf16[16,4,4,864]{3,2,1,0:T(4,128)(2,1)S(1)}, f32[16,4,4,864]{3,2,1,0:T(4,128)}) fusion(f32[16,4,4,864]{3,2,1,0:T(4,128)S(1)} %copy-done, f32[16,4,1,864]{3,2,1,0:T(1,128)} %get-tuple-element.17, f32[16,4,3,864]{3,2,1,0:T(4,128)S(1)} %get-tuple-element.19, f32[864]{0:T(1024)S(1)} %get-tuple-element.28, ...), kind=kLoop, calls=%fused_computation.169 | loop fusion | flops 6856704 | bytes 5550336 | tf_op jit(solution)/shard_map/convert_element_type | solution.py:124
  21.3 10.2 %all-to-all-start = ((bf16[16,8,864]{2,1,0:T(8,128)(2,1)}), bf16[16,8,864]{2,1,0:T(8,128)(2,1)S(1)}, u32[]{:S(2)}, u32[]{:S(2)}) async-start(bf16[16,8,864]{2,1,0:T(8,128)(2,1)} %bitcast.14), calls=%async_computation | async-start | bytes 458752 | tf_op jit(solution)/shard_map/all_to_all | solution.py:134
  32.5 9.9 %all-to-all-done = bf16[16,8,864]{2,1,0:T(8,128)(2,1)S(1)} async-done(((bf16[16,8,864]{2,1,0:T(8,128)(2,1)}), bf16[16,8,864]{2,1,0:T(8,128)(2,1)S(1)}, u32[]{:S(2)}, u32[]{:S(2)}) %all-to-all-start) | async-done | bytes 221216 | tf_op jit(solution)/shard_map/all_to_all | solution.py:134
  43.7 2.5 %convert_bitcast_fusion = bf16[2,8,24,24,24,1]{3,4,2,1,0,5:T(8,128)(2,1)S(1)} fusion(bf16[8,24,24,24,1]{3,2,1,0,4:T(8,128)(2,1)S(1)} %reshape.253, bf16[1,2,24,24]{2,3,0,1:T(8,128)(2,1)S(1)} %get-tuple-element.24, bf16[1,2,24,24]{2,3,0,1:T(8,128)(2,1)S(1)} %get-tuple-element.21), kind=kOutput, calls=%fused_computation.51 | convolution fusion | flops 10842624 | bytes 668160 | tf_op jit(solution)/shard_map/nabz,qzw->qnabw/dot_general | solution.py:69
  46.1 2.5 %fusion.3 = bf16[2,8,24,24,24]{4,3,2,1,0:T(8,128)(2,1)S(1)} fusion(bf16[2,8,24,24,24,1]{3,4,2,1,0,5:T(8,128)(2,1)S(1)} %convert_bitcast_fusion, bf16[1,2,24,24]{2,3,0,1:T(8,128)(2,1)S(1)} %get-tuple-element.21, bf16[1,2,24,24]{2,3,0,1:T(8,128)(2,1)S(1)} %get-tuple-element.24), kind=kOutput, calls=%fused_computation.14 | convolution fusion | flops 21457152 | bytes 889344 | tf_op jit(solution)/shard_map/pnayc,qpyw->qnawc/dot_general | solution.py:69
  48.6 4.0 %fusion.4 = (bf16[2,8,24,24,24]{4,2,3,1,0:T(8,128)(2,1)}, bf16[2,8,24,24,24]{4,2,3,1,0:T(8,128)(2,1)}, bf16[2,8,24,24,24]{4,2,3,1,0:T(8,128)(2,1)S(1)}) fusion(f32[24,24,24]{2,0,1:T(8,128)S(1)} %copy.72, f32[24,24,24]{2,0,1:T(8,128)S(1)} %copy.68, f32[24,24,24]{2,0,1:T(8,128)S(1)} %copy.64, bf16[2,8,24,24,24]{4,3,2,1,0:T(8,128)(2,1)S(1)} %fusion.3, ...), kind=kOutput, calls=%fused_computation.15 | convolution fusion | flops 22563072 | bytes 1939968 | tf_op jit(solution)/shard_map/pnxbc,qpxw->qnwbc/dot_general | solution.py:69
  53.4 3.6 %fusion.9 = f32[8,24,24,24,1]{3,2,4,1,0:T(8,128)} fusion(bf16[2,8,24,24,24,1]{4,2,3,1,0,5:T(8,128)(2,1)S(1)} %fusion.7, bf16[1,24,24]{1,2,0:T(8,128)(2,1)} %copy-done.9, bf16[1,24,24]{1,2,0:T(8,128)(2,1)} %copy-done.8, bf16[1,2,24,24]{2,3,1,0:T(8,128)(2,1)} %get-tuple-element.25, bf16[1,2,24,24]{2,3,1,0:T(8,128)(2,1)S(1)} %get-tuple-element.20), kind=kOutput, calls=%fused_computation.20 | convolution fusion | flops 32082048 | bytes 891648 | tf_op jit(solution)/shard_map/pnabz,pzw->nabw/dot_general | solution.py:69
  57.0 2.5 %fusion.11 = bf16[2,8,24,24,24,1]{4,2,3,1,0,5:T(8,128)(2,1)S(1)} fusion(bf16[2,8,24,24,24]{4,2,3,1,0:T(8,128)(2,1)} %get-tuple-element.10, bf16[1,2,24,24]{2,3,1,0:T(8,128)(2,1)} %get-tuple-element.25, bf16[1,2,24,24]{2,3,1,0:T(8,128)(2,1)S(1)} %get-tuple-element.20), kind=kOutput, calls=%fused_computation.21 | convolution fusion | flops 21464064 | bytes 889344 | tf_op jit(solution)/shard_map/pnxbc,qpxw->qnwbc/dot_general | solution.py:69
  59.5 3.6 %fusion.13 = f32[8,24,24,24,1]{3,2,4,1,0:T(8,128)} fusion(bf16[2,8,24,24,24,1]{4,2,3,1,0,5:T(8,128)(2,1)S(1)} %fusion.11, bf16[1,24,24]{1,2,0:T(8,128)(2,1)} %copy-done.9, bf16[1,24,24]{1,2,0:T(8,128)(2,1)} %copy-done.8, bf16[1,2,24,24]{2,3,1,0:T(8,128)(2,1)} %get-tuple-element.25, bf16[1,2,24,24]{2,3,1,0:T(8,128)(2,1)S(1)} %get-tuple-element.20), kind=kOutput, calls=%fused_computation.23 | convolution fusion | flops 32082048 | bytes 891648 | tf_op jit(solution)/shard_map/pnabz,pzw->nabw/dot_general | solution.py:69
  63.1 2.5 %fusion.15 = bf16[2,8,24,24,24,1]{4,2,3,1,0,5:T(8,128)(2,1)S(1)} fusion(bf16[2,8,24,24,24]{4,2,3,1,0:T(8,128)(2,1)} %get-tuple-element.9, bf16[1,2,24,24]{2,3,1,0:T(8,128)(2,1)} %get-tuple-element.25, bf16[1,2,24,24]{2,3,1,0:T(8,128)(2,1)S(1)} %get-tuple-element.20), kind=kOutput, calls=%fused_computation.24 | convolution fusion | flops 21464064 | bytes 889344 | tf_op jit(solution)/shard_map/pnxbc,qpxw->qnwbc/dot_general | solution.py:69
  65.6 5.1 %fusion.20 = bf16[8,24,24,24]{3,2,1,0:T(8,128)(2,1)} fusion(f32[8,24,24,24,1]{3,2,4,1,0:T(8,128)} %fusion.13, f32[8,24,24,24,1]{3,2,4,1,0:T(8,128)} %fusion.9, bf16[8,24,24,24]{3,2,1,0:T(8,128)(2,1)S(1)} %reshape_squeeze.3, bf16[2,8,24,24,24,1]{4,2,3,1,0,5:T(8,128)(2,1)S(1)} %fusion.15, bf16[1,24,24]{1,2,0:T(8,128)(2,1)} %copy-done.9, ...), kind=kOutput, calls=%fused_computation.29 | convolution fusion | flops 32635008 | bytes 1776384 | tf_op jit(solution)/shard_map/pnabz,pzw->nabw/dot_general | solution.py:69
  70.8 2.1 %convert_element_type.212 = bf16[1,8,16,864]{3,2,1,0:T(8,128)(2,1)S(1)} reshape(bf16[8,24,24,24]{3,2,1,0:T(8,128)(2,1)} %fusion.20) | data formatting | bytes 442368 | tf_op jit(solution)/shard_map/convert_element_type | solution.py:147
  73.0 3.5 %all_to_all.25 = bf16[8,2,1,8,864]{4,3,0,2,1:T(8,128)(2,1)S(1)} all-to-all(bf16[8,2,1,8,864]{4,3,0,2,1:T(8,128)(2,1)S(1)} %copy.77), channel_id=1, replica_groups=mesh['vel_0'=8,'vel_1'=2,'cx'=4,'cy'=4] {'vel_1'}, dimensions={1} | all-to-all | bytes 442368 | tf_op jit(solution)/shard_map/all_to_all | solution.py:48
  77.2 3.4 %all-to-all-start.2 = ((bf16[8,2,1,8,864]{4,3,1,2,0:T(8,128)(2,1)}), bf16[8,2,1,8,864]{4,3,1,2,0:T(8,128)(2,1)S(1)}, u32[]{:S(2)}, u32[]{:S(2)}) async-start(bf16[8,2,1,8,864]{4,3,1,2,0:T(8,128)(2,1)} %copy.78), calls=%async_computation.2 | async-start | bytes 458752 | tf_op jit(solution)/shard_map/all_to_all | solution.py:48
  80.8 11.3 %all-to-all-done.2 = bf16[8,2,1,8,864]{4,3,1,2,0:T(8,128)(2,1)S(1)} async-done(((bf16[8,2,1,8,864]{4,3,1,2,0:T(8,128)(2,1)}), bf16[8,2,1,8,864]{4,3,1,2,0:T(8,128)(2,1)S(1)}, u32[]{:S(2)}, u32[]{:S(2)}) %all-to-all-start.2) | async-done | bytes 221216 | tf_op jit(solution)/shard_map/all_to_all | solution.py:48
  92.2 1.1 %gather_fusion = f32[256,864]{1,0:T(8,128)S(1)} fusion(f32[128,864]{1,0:T(8,128)S(1)} %bitcast_convert_fusion.7, s32[1024]{0:T(1024)S(1)} %pad_clamp_fusion), kind=kCustom, calls=%fused_computation | custom fusion | bytes 1770496 | tf_op jit(solution)/shard_map/gather | solution.py:150
  94.5 1.3 %multiply_add_fusion = f32[16,4,4,864]{3,2,1,0:T(4,128)} fusion(f32[16,4,4,864]{3,2,1,0:T(4,128)S(1)} %copy-done.1, f32[16,4,4,864]{3,2,1,0:T(4,128)S(1)} %gather.6, f32[16,4,4]{2,1,0:T(4,128)S(1)} %copy.53, pred[16,4,4]{2,1,0:T(4,128)(4,1)S(1)} %copy-done.11), kind=kLoop, calls=%fused_computation.79 | loop fusion | flops 663552 | bytes 2655488 | tf_op jit(solution)/shard_map/add | solution.py:152
  (74 shorter events, 10.5 us)
Async XLA Ops:
  0.0 9.7 %copy-start = (f32[16,4,4,864]{3,2,1,0:T(4,128)S(1)}, f32[16,4,4,864]{3,2,1,0:T(4,128)}, u32[]{:S(2)}) copy-start(f32[16,4,4,864]{3,2,1,0:T(4,128)} %param.5) | copy-start | bytes 2654212
  1.6 12.5 %collective-permute-start = (f32[1,4,4,864]{3,2,1,0:T(4,128)}, f32[1,4,4,864]{3,2,1,0:T(4,128)S(1)}, u32[]{:S(2)}, u32[]{:S(2)}) collective-permute-start(f32[1,4,4,864]{3,2,1,0:T(4,128)} %get-tuple-element.15), channel_id=1, source_target_pairs={{0,4},{4,8},{8,12},{12,0},{1,5},{5,9},{9,13},{13,1},{2,6},{6,10},{... | collective-permute-start | bytes 165896 | tf_op jit(solution)/shard_map/ppermute | solution.py:20
  3.7 10.6 %collective-permute-start.1 = (f32[1,4,4,864]{3,2,1,0:T(4,128)}, f32[1,4,4,864]{3,2,1,0:T(4,128)S(1)}, u32[]{:S(2)}, u32[]{:S(2)}) collective-permute-start(f32[1,4,4,864]{3,2,1,0:T(4,128)} %get-tuple-element.14), channel_id=1, source_target_pairs={{4,0},{8,4},{12,8},{0,12},{5,1},{9,5},{13,9},{1,13},{6,2},{10,6},{... | collective-permute-start | bytes 165896 | tf_op jit(solution)/shard_map/ppermute | solution.py:21
  7.0 4.2 %copy-start.12 = (s32[16,4,4]{0,2,1:T(4,128)S(1)}, s32[16,4,4]{0,2,1:T(4,128)}, u32[]{:S(2)}) copy-start(s32[16,4,4]{0,2,1:T(4,128)} %param.6) | copy-start | bytes 3076
  7.0 7.3 %collective-permute-start.2 = (f32[16,1,4,864]{3,2,1,0:T(4,128)}, f32[16,1,4,864]{3,2,1,0:T(4,128)}, u32[]{:S(2)}, u32[]{:S(2)}) collective-permute-start(f32[16,1,4,864]{3,2,1,0:T(4,128)} %get-tuple-element.12), channel_id=1, source_target_pairs={{0,1},{1,2},{2,3},{3,0},{4,5},{5,6},{6,7},{7,4},{8,9},{9,10},{10,1... | collective-permute-start | bytes 663560 | tf_op jit(solution)/shard_map/ppermute | solution.py:20
  8.2 6.1 %collective-permute-start.3 = (f32[16,1,4,864]{3,2,1,0:T(4,128)}, f32[16,1,4,864]{3,2,1,0:T(4,128)}, u32[]{:S(2)}, u32[]{:S(2)}) collective-permute-start(f32[16,1,4,864]{3,2,1,0:T(4,128)} %get-tuple-element.13), channel_id=1, source_target_pairs={{1,0},{2,1},{3,2},{0,3},{5,4},{6,5},{7,6},{4,7},{9,8},{10,9},{11,1... | collective-permute-start | bytes 663560 | tf_op jit(solution)/shard_map/ppermute | solution.py:21
  9.7 2.4 %copy-start.4 = (f32[24,24,24]{2,1,0:T(8,128)S(1)}, f32[24,24,24]{2,1,0:T(8,128)}, u32[]{:S(2)}) copy-start(f32[24,24,24]{2,1,0:T(8,128)} %param.7) | copy-start | bytes 165892
  14.0 0.6 copy-start.10
  14.1 0.6 copy-start.6
  14.3 0.6 copy-start.7
  19.9 11.6 %copy-start.5 = (f32[24,24,24]{2,1,0:T(8,128)S(1)}, f32[24,24,24]{2,1,0:T(8,128)}, u32[]{:S(2)}) copy-start(f32[24,24,24]{2,1,0:T(8,128)} %param.9) | copy-start | bytes 165892
  19.9 11.7 %copy-start.2 = (f32[24,24,24]{2,1,0:T(8,128)S(1)}, f32[24,24,24]{2,1,0:T(8,128)}, u32[]{:S(2)}) copy-start(f32[24,24,24]{2,1,0:T(8,128)} %broadcast_multiply_fusion.2) | copy-start | bytes 165892
  21.3 21.1 %all-to-all-start = ((bf16[16,8,864]{2,1,0:T(8,128)(2,1)}), bf16[16,8,864]{2,1,0:T(8,128)(2,1)S(1)}, u32[]{:S(2)}, u32[]{:S(2)}) async-start(bf16[16,8,864]{2,1,0:T(8,128)(2,1)} %bitcast.14), calls=%async_computation | async-start | bytes 458752 | tf_op jit(solution)/shard_map/all_to_all | solution.py:134
  31.9 10.5 %copy-start.8 = (bf16[1,24,24]{1,2,0:T(8,128)(2,1)}, bf16[1,24,24]{1,2,0:T(8,128)(2,1)S(1)}, u32[]{:S(2)}) copy-start(bf16[1,24,24]{1,2,0:T(8,128)(2,1)S(1)} %get-tuple-element.34) | copy-start | bytes 3460
  31.9 10.5 %copy-start.9 = (bf16[1,24,24]{1,2,0:T(8,128)(2,1)}, bf16[1,24,24]{1,2,0:T(8,128)(2,1)S(1)}, u32[]{:S(2)}) copy-start(bf16[1,24,24]{1,2,0:T(8,128)(2,1)S(1)} %get-tuple-element.35) | copy-start | bytes 3460
  48.6 4.0 %copy-start.3 = (bf16[1,2,24,24]{2,3,1,0:T(8,128)(2,1)S(1)}, bf16[1,2,24,24]{2,3,1,0:T(8,128)(2,1)}, u32[]{:S(2)}) copy-start(bf16[1,2,24,24]{2,3,1,0:T(8,128)(2,1)} %get-tuple-element.25) | copy-start | bytes 6916
  70.8 9.9 %copy-start.13 = (s32[16,4,4]{0,2,1:T(4,128)S(1)}, s32[16,4,4]{0,2,1:T(4,128)}, u32[]{:S(2)}) copy-start(s32[16,4,4]{0,2,1:T(4,128)} %param.6) | copy-start | bytes 3076
  77.2 14.9 %all-to-all-start.2 = ((bf16[8,2,1,8,864]{4,3,1,2,0:T(8,128)(2,1)}), bf16[8,2,1,8,864]{4,3,1,2,0:T(8,128)(2,1)S(1)}, u32[]{:S(2)}, u32[]{:S(2)}) async-start(bf16[8,2,1,8,864]{4,3,1,2,0:T(8,128)(2,1)} %copy.78), calls=%async_computation.2 | async-start | bytes 458752 | tf_op jit(solution)/shard_map/all_to_all | solution.py:48
  92.2 1.4 %copy-start.11 = (pred[16,4,4]{2,1,0:T(4,128)(4,1)S(1)}, pred[16,4,4]{2,1,0:T(4,128)(4,1)}, u32[]{:S(2)}) copy-start(pred[16,4,4]{2,1,0:T(4,128)(4,1)} %copy-done.10) | copy-start | bytes 772
  93.3 1.2 %copy-start.1 = (f32[16,4,4,864]{3,2,1,0:T(4,128)S(1)}, f32[16,4,4,864]{3,2,1,0:T(4,128)}, u32[]{:S(2)}) copy-start(f32[16,4,4,864]{3,2,1,0:T(4,128)} %get-tuple-element.8) | copy-start | bytes 2654212
where the time goes:
time: 96.4 us; the launch traced here: 95.7 us
  matrix products  27.4 us (28%)
  waiting for transfers between devices  21.2 us (22%)
  starting transfers between devices  19.8 us (21%)
  local copies, waits for them, and re-layouts  14.1 us (15%)
  other arithmetic  9.33 us (10%)
  blocking collectives  3.55 us (4%)
    dot_general x9, matrix products, contract(): jnp.einsum(pattern, left_side, right_side, preferred_element_type=jnp.flo...  27.1 us
    all_to_all x1, waiting for transfers between devices, turned_blocks(): out = lax.all_to_all(out, axes[k], k, k, tiled=True)  11.3 us
    all_to_all x1, starting transfers between devices, per_device(): lax.all_to_all(chosen.reshape(groups, capacity // groups, local_vel), VEL...  10.2 us
    all_to_all x1, waiting for transfers between devices, per_device(): lax.all_to_all(chosen.reshape(groups, capacity // groups, local_vel), VEL...  9.88 us
    convert_element_type x1, other arithmetic, per_device(): flattened = read.reshape(block_cells, local_vel).astype(jnp.bfloat16)  4.97 us
    all_to_all x1, blocking collectives, turned_blocks(): out = lax.all_to_all(out, axes[k], k, k, tiled=True)  3.55 us
    all_to_all x1, starting transfers between devices, turned_blocks(): out = lax.all_to_all(out, axes[k], k, k, tiled=True)  3.4 us
    ppermute x2, starting transfers between devices, extended(): lax.ppermute(last, axis, up)  3.33 us
  transfers between devices with their start and end apart: 6, of which 2 were waited for; matrix products, arithmetic and copies ran while one was open for 8% of the time, Pallas kernels for 0%

commit v1 on v0

v1 whole, which is shorter than its diff:
```python
import functools
import math

import jax
import jax.numpy as jnp
import numpy as np
from jax import lax
from jax.experimental import pallas as pl
from jax.experimental.pallas import tpu as pltpu
from jax.sharding import PartitionSpec as P

MESH = pl.DeviceIdType.MESH
F32, BF16 = jnp.float32, jnp.bfloat16
NV, NC = 24, 16
PLANE, HALF, LOCAL = NV * NV, NV * NV // 2, NV * NV * 3 // 2
FREQ = NV * NC
GROUPS, CELLS = 16, 8
ROWS = NV * CELLS
OUTER, MIDDLE = ((0, 384), (512, 352)), ((256, 384),)


def tables():
    jk = np.arange(PLANE)
    bc = np.arange(FREQ)
    turns = (np.outer(jk // NV, bc // NC) + np.outer(jk % NV, bc % NC)) % NV
    keep = (bc % NC <= NV // 2).astype(np.float64)
    twice = np.where((bc % NC == 0) | (bc % NC == NV // 2), 1.0, 2.0) * keep
    cosine = np.round(np.cos(2 * np.pi * turns / NV), 12)
    sine = np.round(np.sin(2 * np.pi * turns / NV), 12)
    forward = np.concatenate([cosine * keep, -sine * keep], 1)
    inverse = np.concatenate([(cosine * twice).T, (-sine * twice).T], 0)
    turns = np.outer(np.arange(NV), np.arange(NV)) % NV
    eye = np.eye(CELLS)
    along_x = np.concatenate(
        [
            np.kron(np.round(np.cos(2 * np.pi * turns / NV), 12), eye),
            np.kron(np.round(np.sin(2 * np.pi * turns / NV), 12), eye),
        ],
        0,
    )
    return tuple(jnp.asarray(t, dtype=BF16) for t in (forward, inverse, along_x))


def iota(shape, dim):
    return lax.broadcasted_iota(jnp.int32, shape, dim)


def dot(a, b):
    return jnp.dot(a, b, preferred_element_type=F32)


def kernel(
    dist, level, sym, forward_hbm, inverse_hbm, along_hbm, out,
    ext, read, send, recv, field, packed, result, forward, inverse, along,
    local_sem, table_sem, out_sem, face_send, face_recv, send_sem, recv_sem, back_send, back_recv,
):
    me = lax.axis_index("vel")
    my_x, my_y = lax.axis_index("cx"), lax.axis_index("cy")
    nx, ny = lax.axis_size("cx"), lax.axis_size("cy")
    x_low, x_high = {"cx": lax.rem(my_x + nx - 1, nx)}, {"cx": lax.rem(my_x + 1, nx)}
    y_low, y_high = {"cy": lax.rem(my_y + ny - 1, ny)}, {"cy": lax.rem(my_y + 1, ny)}
    falling = me < GROUPS // 2
    even = lax.rem(me, 2) == 0

    loads = [
        pltpu.make_async_copy(dist.at[0:8], ext.at[1:9, 1:5, 0:4], local_sem.at[0]),
        pltpu.make_async_copy(dist.at[8:16], ext.at[1:9, 1:5, 4:8], local_sem.at[1]),
        pltpu.make_async_copy(dist.at[8], ext.at[9, 1:5, 0:4], local_sem.at[2]),
        pltpu.make_async_copy(dist.at[7], ext.at[0, 1:5, 4:8], local_sem.at[3]),
    ]
    for load in loads:
        load.start()
    table_loads = [
        pltpu.make_async_copy(src, dst, table_sem.at[k])
        for k, (src, dst) in enumerate(
            ((forward_hbm, forward), (inverse_hbm, inverse), (along_hbm, along))
        )
    ]
    for load in table_loads:
        load.start()

    barrier = pltpu.get_barrier_semaphore()
    for there in (x_low, x_high, y_low, y_high):
        pl.semaphore_signal(barrier, inc=1, device_id=there, device_id_type=MESH)
    order = [8 + (k + 1) // 2 * (-1) ** k for k in range(GROUPS - 1)]
    for d in order:
        pl.semaphore_signal(
            barrier, inc=1, device_id={"vel": lax.rem(me + d, GROUPS)}, device_id_type=MESH
        )
    pl.semaphore_wait(barrier, GROUPS - 1 + 4)

    def remote(src, dst, send_at, recv_at, there):
        return pltpu.make_async_remote_copy(
            src_ref=src, dst_ref=dst, send_sem=send_at, recv_sem=recv_at,
            device_id=there, device_id_type=MESH,
        )

    def x_copy(up):
        if up:
            return remote(
                dist.at[0], ext.at[9, 1:5, 4:8], face_send.at[0], face_recv.at[0], x_low
            )
        return remote(dist.at[15], ext.at[0, 1:5, 0:4], face_send.at[0], face_recv.at[0], x_high)

    def y_copies(is_even):
        copies, at = [], 1
        for upper, segments in ((is_even, OUTER), (not is_even, MIDDLE)):
            for first, width in segments:
                for s in range(2):
                    lanes = pl.ds(first, width)
                    copies.append(
                        remote(
                            dist.at[8 * s : 8 * s + 8, 0 if upper else 3, :, lanes],
                            ext.at[1:9, 5 if upper else 0, 4 * s : 4 * s + 4, lanes],
                            face_send.at[at], face_recv.at[at], y_low if upper else y_high,
                        )
                    )
                    at += 1
        return copies

    for case in (True, False):

        @pl.when(even == case)
        def _():
            for copy in y_copies(case):
                copy.start()

    for case in (True, False):

        @pl.when(falling == case)
        def _():
            x_copy(case).start()

    levels = jnp.concatenate([level[y] for y in range(4)], axis=0).astype(F32).astype(BF16)
    r = iota((16, 256), 1)
    row = iota((16, 256), 0)
    x_hot = (row == lax.rem(r // 4, 2) * 8 + r // 32).astype(F32).astype(BF16)
    yz_hot = row == lax.rem(r // 8, 4) * 4 + lax.rem(r, 4)
    spread = dot(levels, x_hot)
    level_row = jnp.sum(jnp.where(yz_hot, spread, 0.0), axis=0, keepdims=True)
    active = (level_row > 0.5).astype(F32)
    upto = (iota((256, 256), 0) <= iota((256, 256), 1)).astype(F32).astype(BF16)
    slot = dot(jnp.broadcast_to(active, (8, 256)).astype(BF16), upto)[0:1] - 1.0
    hot = (
        (iota((128, 256), 0).astype(F32) == slot) & (jnp.broadcast_to(active, (128, 256)) > 0.5)
    ).astype(F32)
    picker = hot.astype(BF16)
    placer = (hot * (0.25 * level_row)).astype(BF16)

    lane = iota((1, LOCAL), 1) + me * LOCAL

    def speed(index):
        return 0.3 * (2.0 * index.astype(F32) - (NV - 1)) / (NV - 1)

    c_x = speed(lane // PLANE)
    c_y = speed(lax.rem(lane // NV, NV))
    c_z = speed(lax.rem(lane, NV))
    shape = (8, LOCAL)
    a_x, a_y, a_z = (jnp.broadcast_to(jnp.abs(c), shape) for c in (c_x, c_y, c_z))
    up_y, up_z = (jnp.broadcast_to(c, shape) > 0.0 for c in (c_y, c_z))
    z_at = lax.rem(iota(shape, 0), 4)
    first_z, last_z = z_at == 0, z_at == 3
    step_x = jnp.where(falling, 1, -1)

    for load in loads:
        load.wait()
    for case in (True, False):

        @pl.when(even == case)
        def _():
            for copy in y_copies(case):
                copy.wait()

    for case in (True, False):

        @pl.when(falling == case)
        def _():
            x_copy(case).wait()

    def plane(x, _):
        for y in range(4):
            f = ext[x + 1, y + 1]
            flux = a_x * (f - ext[x + 1 + step_x, y + 1])
            flux = flux + a_y * (f - jnp.where(up_y, ext[x + 1, y], ext[x + 1, y + 2]))
            low = jnp.where(first_z, pltpu.roll(f, 5, 0), pltpu.roll(f, 1, 0))
            high = jnp.where(last_z, pltpu.roll(f, 3, 0), pltpu.roll(f, 7, 0))
            flux = flux + a_z * (f - jnp.where(up_z, low, high))
            read[x, y] = f - flux
        return 0

    lax.fori_loop(0, 8, plane, 0)

    chosen = dot(picker, read[...].reshape(256, LOCAL).astype(BF16))
    send[...] = chosen.astype(BF16).reshape(GROUPS, CELLS, LOCAL)

    def exchange(there, send_sems, recv_sems):
        peer = lax.rem(me + there, GROUPS)
        return remote(
            send.at[peer], recv.at[me], send_sems.at[peer], recv_sems.at[me], {"vel": peer}
        )

    def arrived(d, recv_sems):
        peer = lax.rem(me + d, GROUPS)
        return remote(
            send.at[peer], recv.at[peer], send_sem.at[peer], recv_sems.at[peer], {"vel": peer}
        )

    for d in order:
        exchange(d, send_sem, recv_sem).start()
    recv[me] = send[me]
    for load in table_loads:
        load.wait()
    for d in order:
        arrived(d, recv_sem).wait_recv()

    for p in range(GROUPS // 2):
        left, right = recv[2 * p].astype(F32), recv[2 * p + 1].astype(F32)
        at = 3 * p * CELLS
        field[at : at + 8] = left[:, :PLANE]
        field[at + 8 : at + 16, :HALF] = left[:, PLANE:]
        field[at + 8 : at + 16, HALF:] = right[:, :HALF]
        field[at + 16 : at + 24] = right[:, HALF:]

    cells = field[...]
    section = dot(cells.astype(BF16), forward[...]).astype(BF16)
    turned = dot(along[...], section)
    spec_re = turned[:ROWS, :FREQ] + turned[ROWS:, FREQ:]
    spec_im = turned[:ROWS, FREQ:] - turned[ROWS:, :FREQ]
    filtered = []
    for k in range(3):
        weights = jnp.broadcast_to(
            sym[k * NV : (k + 1) * NV][:, None, :], (NV, CELLS, FREQ)
        ).reshape(ROWS, FREQ)
        weighted = jnp.concatenate([spec_re * weights, spec_im * weights], axis=1).astype(BF16)
        turned = dot(along[...], weighted)
        back = jnp.concatenate(
            [
                turned[:ROWS, :FREQ] - turned[ROWS:, FREQ:],
                turned[:ROWS, FREQ:] + turned[ROWS:, :FREQ],
            ],
            axis=1,
        ).astype(BF16)
        filtered.append(dot(back, inverse[...]))
    field[...] = filtered[0] * filtered[1] - cells * filtered[2]

    for d in order:
        peer = lax.rem(me + d, GROUPS)
        exchange(d, send_sem, recv_sem).wait_send()
    for p in range(GROUPS // 2):
        at = 3 * p * CELLS
        send[2 * p] = jnp.concatenate(
            [field[at : at + 8], field[at + 8 : at + 16, :HALF]], axis=1
        ).astype(BF16)
        send[2 * p + 1] = jnp.concatenate(
            [field[at + 8 : at + 16, HALF:], field[at + 16 : at + 24]], axis=1
        ).astype(BF16)

    def give_back(d):
        peer = lax.rem(me + d, GROUPS)
        return remote(
            send.at[peer], packed.at[me], back_send.at[peer], back_recv.at[me], {"vel": peer}
        )

    def came_back(d):
        peer = lax.rem(me + d, GROUPS)
        return remote(
            send.at[peer], packed.at[peer], back_send.at[peer], back_recv.at[peer], {"vel": peer}
        )

    for d in order:
        give_back(d).start()
    packed[me] = send[me]
    for d in order:
        came_back(d).wait_recv()

    rates = lax.dot_general(
        placer, packed[...].reshape(GROUPS * CELLS, LOCAL), (((0,), (0,)), ((), ())),
        preferred_element_type=F32,
    )
    result[...] = read[...] + rates.reshape(8, 4, 8, LOCAL)
    stores = [
        pltpu.make_async_copy(result.at[:, :, 0:4], out.at[0:8], out_sem.at[0]),
        pltpu.make_async_copy(result.at[:, :, 4:8], out.at[8:16], out_sem.at[1]),
    ]
    for store in stores:
        store.start()
    for d in order:
        give_back(d).wait_send()
    for store in stores:
        store.wait()


def frequency_weights(kernels):
    k = jnp.stack(kernels)
    other = jnp.roll(jnp.flip(k, (1, 2, 3)), 1, (1, 2, 3))
    k = (k + other)[..., : NV // 2 + 1] * (0.5 / float(NV**3))
    k = jnp.pad(k, ((0, 0), (0, 0), (0, 0), (0, NC - NV // 2 - 1)))
    return k.reshape(3 * NV, FREQ)


def per_device(distribution, refine_level, gain_one, gain_two, loss_kernel):
    sym = frequency_weights((gain_one, gain_two, loss_kernel))
    forward, inverse, along = tables()
    anywhere = pl.BlockSpec(memory_space=pl.ANY)
    vmem = pl.BlockSpec(memory_space=pltpu.VMEM)
    dma = pltpu.SemaphoreType.DMA
    return pl.pallas_call(
        kernel,
        out_shape=jax.ShapeDtypeStruct(distribution.shape, F32),
        in_specs=[anywhere, vmem, vmem, anywhere, anywhere, anywhere],
        out_specs=anywhere,
        scratch_shapes=[
            pltpu.VMEM((10, 6, 8, LOCAL), F32),
            pltpu.VMEM((8, 4, 8, LOCAL), F32),
            pltpu.VMEM((GROUPS, CELLS, LOCAL), BF16),
            pltpu.VMEM((GROUPS, CELLS, LOCAL), BF16),
            pltpu.VMEM((ROWS, PLANE), F32),
            pltpu.VMEM((GROUPS, CELLS, LOCAL), BF16),
            pltpu.VMEM((8, 4, 8, LOCAL), F32),
            pltpu.VMEM((PLANE, 2 * FREQ), BF16),
            pltpu.VMEM((2 * FREQ, PLANE), BF16),
            pltpu.VMEM((2 * ROWS, ROWS), BF16),
            dma((4,)), dma((3,)), dma((2,)), dma((7,)), dma((7,)),
            dma((GROUPS,)), dma((GROUPS,)), dma((GROUPS,)), dma((GROUPS,)),
        ],
        compiler_params=pltpu.CompilerParams(
            collective_id=0, has_side_effects=True, vmem_limit_bytes=48 << 20
        ),
    )(distribution, refine_level.transpose(1, 2, 0), sym, forward, inverse, along)


def solution(mesh):
    in_specs = (P("cx", "cy", None, "vel"), P("cx", "cy", None), P(), P(), P())
    return jax.shard_map(
        per_device, mesh=mesh, in_specs=in_specs,
        out_specs=P("cx", "cy", None, "vel"), check_vma=False,
    )
```

time: 96.4 us -> 41.7 us (0.43)
  Pallas kernels: 0 us -> 35.1 us
  matrix products: 27.4 us -> 0 us
  waiting for transfers between devices: 21.2 us -> 0 us
  starting transfers between devices: 19.8 us -> 0 us
  local copies, waits for them, and re-layouts: 14.1 us -> 4.72 us
  other arithmetic: 9.33 us -> 1.68 us
  blocking collectives: 3.55 us -> 0 us
    pallas_call x0 -> x1, Pallas kernels: none -> 35.1 us  [per_device(): pl.pallas_call(kernel, out_shape=jax.ShapeDtypeStruct(distribution.shape,...]
    dot_general x10 -> x0, matrix products: 27.4 us -> none  [the longest x9 27.1 us: contract(): jnp.einsum(pattern, left_side, right_side, preferred_element_type=jnp.flo...]
    all_to_all x2 -> x0, waiting for transfers between devices: 21.2 us -> none  [the longest x1 11.3 us: turned_blocks(): out = lax.all_to_all(out, axes[k], k, k, tiled=True)]
    all_to_all x2 -> x0, starting transfers between devices: 13.6 us -> none  [the longest x1 10.2 us: per_device(): lax.all_to_all(chosen.reshape(groups, capacity // groups, local_vel), VEL...]
    ppermute x4 -> x0, starting transfers between devices: 6.23 us -> none  [the longest x2 3.33 us: extended(): lax.ppermute(last, axis, up)]
    convert_element_type x3 -> x0, other arithmetic: 5.03 us -> none  [the longest x1 4.97 us: per_device(): flattened = read.reshape(block_cells, local_vel).astype(jnp.bfloat16)]
    slice x4 -> x5, local copies, waits for them, and re-layouts: 4.93 us -> 1.28 us  [frequency_weights(): other = jnp.roll(jnp.flip(k, (1, 2, 3)), 1, (1, 2, 3))]
    all_to_all x1 -> x0, blocking collectives: 3.55 us -> none  [turned_blocks(): out = lax.all_to_all(out, axes[k], k, k, tiled=True)]
  transfers between devices with their start and end apart: 6 -> 0, of which waited for: 2 -> 0; matrix products, arithmetic and copies ran while one was open for 8% -> 0% of each run, Pallas kernels for 0% -> 0%
where the time goes in v1:
time: 41.7 us; the launch traced here: 41.6 us
  Pallas kernels  35.1 us (84%)
  local copies, waits for them, and re-layouts  4.72 us (11%)
  other arithmetic  1.68 us (4%)
    pallas_call x1, Pallas kernels, per_device(): pl.pallas_call(kernel, out_shape=jax.ShapeDtypeStruct(distribution.shape,...  35.1 us
    reshape x1, local copies, waits for them, and re-layouts, frequency_weights(): return k.reshape(3 * NV, FREQ)  1.52 us
    slice x5, local copies, waits for them, and re-layouts, frequency_weights(): other = jnp.roll(jnp.flip(k, (1, 2, 3)), 1, (1, 2, 3))  1.28 us
    another operation x1, other arithmetic, frequency_weights(): k = jnp.stack(kernels)  1.2 us
    pad x1, local copies, waits for them, and re-layouts, frequency_weights(): k = jnp.pad(k, ((0, 0), (0, 0), (0, 0), (0, NC - NV // 2 - 1)))  0.97 us
    unnamed x11, local copies, waits for them, and re-layouts  0.95 us

profile of v1, /device:TPU:1, one launch (start us, length us, event | category | flops | bytes accessed | tf_op | source)
XLA Modules:
  0.0 41.6 jit_solution(14482191507372187122)
XLA Ops:
  0.0 1.2 %pad_maximum_fusion.3 = f32[3,24,24,24]{3,2,1,0:T(8,128)S(1)} fusion(f32[1,24,24,24]{3,2,1,0:T(8,128)} %bitcast.9, f32[1,24,24,24]{3,2,1,0:T(8,128)} %bitcast.10, f32[1,24,24,24]{3,2,1,0:T(8,128)} %bitcast.11), kind=kLoop, calls=%fused_computation.6 | loop fusion | flops 82944 | bytes 331776 | tf_op jit(solution)/shard_map/stack | solution.py:294
  1.2 0.1 slice.34
  1.3 0.1 slice.43
  1.4 0.8 %slice.36 = f32[3,23,24,24]{3,2,1,0:T(8,128)S(1)} reverse(f32[3,23,24,24]{3,2,1,0:T(8,128)S(1)} %slice.43), dimensions={1,2,3} | reverse | bytes 317952 | tf_op jit(solution)/shard_map/jit(_roll_static)/slice | solution.py:295
  2.2 0.1 fusion.1
  2.4 0.3 slice.44
  2.6 0.0 copy-start.2
  2.7 0.3 fusion
  3.0 0.0 copy-start
  3.0 0.0 copy-start.3
  3.0 1.0 %pad.4 = f32[3,24,24,16]{3,2,1,0:T(8,128)} pad(f32[3,24,24,13]{3,2,1,0:T(8,128)S(1)} %fusion, f32[]{:T(128)} %constant.10.clone.1), padding=0_0x0_0x0_0x0_3 | pad | bytes 200452 | tf_op jit(solution)/shard_map/jit(_pad)/pad | solution.py:297
  4.0 0.0 copy-start.1
  4.0 0.0 copy-start.4
  4.0 1.5 %reshape.3.sym = f32[72,384]{1,0:T(8,128)S(1)} reshape(f32[3,24,24,16]{3,2,1,0:T(8,128)} %pad.4) | data formatting | bytes 221184 | tf_op jit(solution)/shard_map/reshape | solution.py:298
  5.5 0.0 copy-done.2
  5.5 0.0 copy-done
  5.6 0.0 copy-done.3
  5.6 0.0 copy-done.1
  5.6 0.0 copy-done.4
  5.6 35.1 %shard_map.82 = f32[16,4,4,864]{3,2,1,0:T(4,128)S(1)} custom-call(f32[16,4,4,864]{3,2,1,0:T(4,128)S(1)} %copy-done.1, s32[4,4,16]{2,1,0:T(4,128)S(1)} %bitcast.7, f32[72,384]{1,0:T(8,128)S(1)} %reshape.3.sym, bf16[576,768]{1,0:T(8,128)(2,1)S(1)} %copy-done.2, bf16[768,576]{1,0:T(8,128)(2,1)S(1)} %copy-done, bf16[384,192]{1,0:T(8,128)(2,1)S(1)} %copy-done.3), custom_call_target="tpu_custom_call" | custom-call | tf_op jit(solution)/shard_map/pallas_call | solution.py:307
  40.7 0.9 %copy.10 = f32[16,4,4,864]{3,2,1,0:T(4,128)} copy(f32[16,4,4,864]{3,2,1,0:T(4,128)S(1)} %shard_map.82) | data formatting | bytes 1769472
  (1 shorter events, 0.0 us)
Async XLA Ops:
  2.6 2.9 %copy-start.2 = (bf16[576,768]{1,0:T(8,128)(2,1)S(1)}, bf16[576,768]{1,0:T(8,128)(2,1)}, u32[]{:S(2)}) copy-start(bf16[576,768]{1,0:T(8,128)(2,1)} %constant.11.clone.forward_hbm) | copy-start | bytes 2654212
  3.0 2.5 %copy-start = (bf16[768,576]{1,0:T(8,128)(2,1)S(1)}, bf16[768,576]{1,0:T(8,128)(2,1)}, u32[]{:S(2)}) copy-start(bf16[768,576]{1,0:T(8,128)(2,1)} %constant.12.clone.inverse_hbm) | copy-start | bytes 2654212
  3.0 2.5 %copy-start.3 = (bf16[384,192]{1,0:T(8,128)(2,1)S(1)}, bf16[384,192]{1,0:T(8,128)(2,1)}, u32[]{:S(2)}) copy-start(bf16[384,192]{1,0:T(8,128)(2,1)} %constant.13.clone.along_hbm) | copy-start | bytes 442372
  4.0 1.6 %copy-start.1 = (f32[16,4,4,864]{3,2,1,0:T(4,128)S(1)}, f32[16,4,4,864]{3,2,1,0:T(4,128)}, u32[]{:S(2)}) copy-start(f32[16,4,4,864]{3,2,1,0:T(4,128)} %dist.1) | copy-start | bytes 2654212
  4.0 1.6 %copy-start.4 = (s32[16,4,4]{0,2,1:T(4,128)S(1)}, s32[16,4,4]{0,2,1:T(4,128)}, u32[]{:S(2)}) copy-start(s32[16,4,4]{0,2,1:T(4,128)} %param.9) | copy-start | bytes 3076

commit v2 on v1

--- a/solution.py
+++ b/solution.py
@@ -16,7 +16,8 @@
 FREQ = NV * NC
 GROUPS, CELLS = 16, 8
 ROWS = NV * CELLS
-OUTER, MIDDLE = ((0, 384), (512, 352)), ((256, 384),)
+SEGMENTS = ((0, 384), (512, 352), (256, 384))
+SEG = 384
 
 
 def tables():
@@ -50,9 +51,9 @@
 
 
 def kernel(
-    dist, level, sym, forward_hbm, inverse_hbm, along_hbm, out,
-    ext, read, send, recv, field, packed, result, forward, inverse, along,
-    local_sem, table_sem, out_sem, face_send, face_recv, send_sem, recv_sem, back_send, back_recv,
+    dist, level_hbm, kernel_a, kernel_b, kernel_c, forward_hbm, inverse_hbm, along_hbm, out,
+    ext, face, halo, read, send, recv, field, packed, forward, inverse, along, raw, spread, sym, level,
+    local_sem, table_sem, hop_sem, face_send, face_recv, send_sem, recv_sem, back_send, back_recv,
 ):
     me = lax.axis_index("vel")
     my_x, my_y = lax.axis_index("cx"), lax.axis_index("cy")
@@ -63,31 +64,37 @@
     even = lax.rem(me, 2) == 0
 
     loads = [
-        pltpu.make_async_copy(dist.at[0:8], ext.at[1:9, 1:5, 0:4], local_sem.at[0]),
-        pltpu.make_async_copy(dist.at[8:16], ext.at[1:9, 1:5, 4:8], local_sem.at[1]),
-        pltpu.make_async_copy(dist.at[8], ext.at[9, 1:5, 0:4], local_sem.at[2]),
-        pltpu.make_async_copy(dist.at[7], ext.at[0, 1:5, 4:8], local_sem.at[3]),
+        pltpu.make_async_copy(
+            dist.at[8 * s : 8 * s + 8, y], ext.at[1:9, y + 1, 4 * s : 4 * s + 4], local_sem.at[2 * y + s]
+        )
+        for y in (0, 3, 1, 2)
+        for s in range(2)
+    ]
+    loads += [
+        pltpu.make_async_copy(dist.at[8], ext.at[9, 1:5, 0:4], local_sem.at[8]),
+        pltpu.make_async_copy(dist.at[7], ext.at[0, 1:5, 4:8], local_sem.at[9]),
+        pltpu.make_async_copy(level_hbm, level, local_sem.at[10]),
     ]
     for load in loads:
         load.start()
     table_loads = [
         pltpu.make_async_copy(src, dst, table_sem.at[k])
         for k, (src, dst) in enumerate(
-            ((forward_hbm, forward), (inverse_hbm, inverse), (along_hbm, along))
+            (
+                (forward_hbm, forward), (inverse_hbm, inverse), (along_hbm, along),
+                (kernel_a, raw.at[0:PLANE]), (kernel_b, raw.at[PLANE : 2 * PLANE]),
+                (kernel_c, raw.at[2 * PLANE : 3 * PLANE]),
+            )
         )
     ]
-    for load in table_loads:
-        load.start()
 
     barrier = pltpu.get_barrier_semaphore()
-    for there in (x_low, x_high, y_low, y_high):
+    twin = me + 1 - 2 * lax.rem(me, 2)
+    near = [twin] + [lax.rem(m + d, GROUPS) for m in (me, twin) for d in (2, GROUPS - 2)]
+    beside = [x_low, x_high, y_low, y_high] + [{"vel": v} for v in near]
+    for there in beside:
         pl.semaphore_signal(barrier, inc=1, device_id=there, device_id_type=MESH)
     order = [8 + (k + 1) // 2 * (-1) ** k for k in range(GROUPS - 1)]
-    for d in order:
-        pl.semaphore_signal(
-            barrier, inc=1, device_id={"vel": lax.rem(me + d, GROUPS)}, device_id_type=MESH
-        )
-    pl.semaphore_wait(barrier, GROUPS - 1 + 4)
 
     def remote(src, dst, send_at, recv_at, there):
         return pltpu.make_async_remote_copy(
@@ -103,21 +110,24 @@
         return remote(dist.at[15], ext.at[0, 1:5, 0:4], face_send.at[0], face_recv.at[0], x_high)
 
     def y_copies(is_even):
-        copies, at = [], 1
-        for upper, segments in ((is_even, OUTER), (not is_even, MIDDLE)):
-            for first, width in segments:
-                for s in range(2):
-                    lanes = pl.ds(first, width)
-                    copies.append(
-                        remote(
-                            dist.at[8 * s : 8 * s + 8, 0 if upper else 3, :, lanes],
-                            ext.at[1:9, 5 if upper else 0, 4 * s : 4 * s + 4, lanes],
-                            face_send.at[at], face_recv.at[at], y_low if upper else y_high,
-                        )
-                    )
-                    at += 1
-        return copies
-
+        outer = remote(
+            face.at[0:2], halo.at[0:2], face_send.at[1], face_recv.at[1],
+            y_low if is_even else y_high,
+        )
+        middle = remote(
+            face.at[2], halo.at[2], face_send.at[2], face_recv.at[2],
+            y_high if is_even else y_low,
+        )
+        return outer, middle
+
+    for load in loads[:4]:
+        load.wait()
+    outer_y = jnp.where(even, 1, 4)
+    for k, (first, width) in enumerate(SEGMENTS):
+        y = 5 - outer_y if k == 2 else outer_y
+        face[k, :, 0:width] = ext[1:9, y, :, first : first + width].reshape(64, width).astype(BF16)
+
+    pl.semaphore_wait(barrier, len(beside))
     for case in (True, False):
 
         @pl.when(even == case)
@@ -131,13 +141,26 @@
         def _():
             x_copy(case).start()
 
+    for load in table_loads:
+        load.start()
+    for k in range(3):
+        for side, d in enumerate((2, GROUPS - 2)):
+            pl.semaphore_signal(
+                hop_sem.at[2 * k + side], inc=1, device_id={"vel": lax.rem(me + d, GROUPS)},
+                device_id_type=MESH,
+            )
+        for side in range(2):
+            pl.semaphore_wait(hop_sem.at[2 * k + side], 1)
+
+    for load in loads[4:]:
+        load.wait()
     levels = jnp.concatenate([level[y] for y in range(4)], axis=0).astype(F32).astype(BF16)
     r = iota((16, 256), 1)
     row = iota((16, 256), 0)
     x_hot = (row == lax.rem(r // 4, 2) * 8 + r // 32).astype(F32).astype(BF16)
     yz_hot = row == lax.rem(r // 8, 4) * 4 + lax.rem(r, 4)
-    spread = dot(levels, x_hot)
-    level_row = jnp.sum(jnp.where(yz_hot, spread, 0.0), axis=0, keepdims=True)
+    by_yz = dot(levels, x_hot)
+    level_row = jnp.sum(jnp.where(yz_hot, by_yz, 0.0), axis=0, keepdims=True)
     active = (level_row > 0.5).astype(F32)
     upto = (iota((256, 256), 0) <= iota((256, 256), 1)).astype(F32).astype(BF16)
     slot = dot(jnp.broadcast_to(active, (8, 256)).astype(BF16), upto)[0:1] - 1.0
@@ -162,14 +185,17 @@
     first_z, last_z = z_at == 0, z_at == 3
     step_x = jnp.where(falling, 1, -1)
 
-    for load in loads:
-        load.wait()
     for case in (True, False):
 
         @pl.when(even == case)
         def _():
             for copy in y_copies(case):
                 copy.wait()
+
+    outer_halo = jnp.where(even, 5, 0)
+    for k, (first, width) in enumerate(SEGMENTS):
+        y = 5 - outer_halo if k == 2 else outer_halo
+        ext[1:9, y, :, first : first + width] = halo[k, :, 0:width].astype(F32).reshape(8, 8, width)
 
     for case in (True, False):
 
@@ -210,6 +236,25 @@
     recv[me] = send[me]
     for load in table_loads:
         load.wait()
+
+    for b in range(NV):
+        spread[:, NV * b : NV * b + NV] = raw[pl.ds(b, 3 * NV, stride=NV), :]
+    high = spread[...].astype(BF16)
+    parts = jnp.concatenate([high, (spread[...] - high.astype(F32)).astype(BF16)], axis=0)
+    at = iota((6 * NV, 6 * NV), 0)
+    a_at = lax.rem(at, NV)
+    turn = (iota((6 * NV, 6 * NV), 1) == at - a_at + lax.rem(NV - a_at, NV)).astype(F32).astype(BF16)
+    turned = dot(turn, parts).astype(BF16)
+    lane_b, lane_c = iota((1, FREQ), 1) // NC, lax.rem(iota((1, FREQ), 1), NC)
+    used = lane_c <= NV // 2
+    same = jnp.where(used, lane_b * NV + lane_c, -1)
+    other = jnp.where(used, lax.rem(NV - lane_b, NV) * NV + lax.rem(NV - lane_c, NV), -1)
+    pick = iota((PLANE, FREQ), 0)
+    both = dot(parts, (pick == same).astype(F32).astype(BF16)) + dot(
+        turned, (pick == other).astype(F32).astype(BF16)
+    )
+    sym[...] = (both[: 3 * NV] + both[3 * NV :]) * (0.5 / float(NV**3))
+
     for d in order:
         arrived(d, recv_sem).wait_recv()
 
@@ -277,56 +322,51 @@
         placer, packed[...].reshape(GROUPS * CELLS, LOCAL), (((0,), (0,)), ((), ())),
         preferred_element_type=F32,
     )
-    result[...] = read[...] + rates.reshape(8, 4, 8, LOCAL)
-    stores = [
-        pltpu.make_async_copy(result.at[:, :, 0:4], out.at[0:8], out_sem.at[0]),
-        pltpu.make_async_copy(result.at[:, :, 4:8], out.at[8:16], out_sem.at[1]),
-    ]
-    for store in stores:
-        store.start()
+    evolved = read[...] + rates.reshape(8, 4, 8, LOCAL)
+    for part in range(2):
+        out[8 * part : 8 * part + 8] = evolved[:, :, 4 * part : 4 * part + 4]
     for d in order:
         give_back(d).wait_send()
-    for store in stores:
-        store.wait()
-
-
-def frequency_weights(kernels):
-    k = jnp.stack(kernels)
-    other = jnp.roll(jnp.flip(k, (1, 2, 3)), 1, (1, 2, 3))
-    k = (k + other)[..., : NV // 2 + 1] * (0.5 / float(NV**3))
-    k = jnp.pad(k, ((0, 0), (0, 0), (0, 0), (0, NC - NV // 2 - 1)))
-    return k.reshape(3 * NV, FREQ)
+
+
+def in_hbm(array):
+    return pltpu.with_memory_space_constraint(array, pltpu.MemorySpace.HBM)
 
 
 def per_device(distribution, refine_level, gain_one, gain_two, loss_kernel):
-    sym = frequency_weights((gain_one, gain_two, loss_kernel))
     forward, inverse, along = tables()
-    anywhere = pl.BlockSpec(memory_space=pl.ANY)
+    kernels = [k.reshape(PLANE, NV) for k in (gain_one, gain_two, loss_kernel)]
+    hbm = pl.BlockSpec(memory_space=pltpu.MemorySpace.HBM)
     vmem = pl.BlockSpec(memory_space=pltpu.VMEM)
     dma = pltpu.SemaphoreType.DMA
     return pl.pallas_call(
         kernel,
-        out_shape=jax.ShapeDtypeStruct(distribution.shape, F32),
-        in_specs=[anywhere, vmem, vmem, anywhere, anywhere, anywhere],
-        out_specs=anywhere,
+        out_shape=pltpu.VMEM(distribution.shape, F32),
+        in_specs=[hbm] * 8,
+        out_specs=vmem,
         scratch_shapes=[
             pltpu.VMEM((10, 6, 8, LOCAL), F32),
+            pltpu.VMEM((3, 64, SEG), BF16),
+            pltpu.VMEM((3, 64, SEG), BF16),
             pltpu.VMEM((8, 4, 8, LOCAL), F32),
             pltpu.VMEM((GROUPS, CELLS, LOCAL), BF16),
             pltpu.VMEM((GROUPS, CELLS, LOCAL), BF16),
             pltpu.VMEM((ROWS, PLANE), F32),
             pltpu.VMEM((GROUPS, CELLS, LOCAL), BF16),
-            pltpu.VMEM((8, 4, 8, LOCAL), F32),
             pltpu.VMEM((PLANE, 2 * FREQ), BF16),
             pltpu.VMEM((2 * FREQ, PLANE), BF16),
             pltpu.VMEM((2 * ROWS, ROWS), BF16),
-            dma((4,)), dma((3,)), dma((2,)), dma((7,)), dma((7,)),
+            pltpu.VMEM((3 * PLANE, NV), F32),
+            pltpu.VMEM((3 * NV, PLANE), F32),
+            pltpu.VMEM((3 * NV, FREQ), F32),
+            pltpu.VMEM((4, 4, 16), jnp.int32),
+            dma((11,)), dma((6,)), pltpu.SemaphoreType.REGULAR((6,)), dma((3,)), dma((3,)),
             dma((GROUPS,)), dma((GROUPS,)), dma((GROUPS,)), dma((GROUPS,)),
         ],
         compiler_params=pltpu.CompilerParams(
             collective_id=0, has_side_effects=True, vmem_limit_bytes=48 << 20
         ),
-    )(distribution, refine_level.transpose(1, 2, 0), sym, forward, inverse, along)
+    )(*map(in_hbm, (distribution, refine_level.transpose(1, 2, 0), *kernels, forward, inverse, along)))
 
 
 def solution(mesh):

time: 41.7 us -> 32.4 us (0.78)
  local copies, waits for them, and re-layouts: 4.72 us -> 0.93 us
  Pallas kernels: 35.1 us -> 31.4 us
  other arithmetic: 1.68 us -> 0 us
    pallas_call x1, Pallas kernels: 35.1 us -> 31.4 us  [per_device(): pl.pallas_call(kernel, out_shape=pltpu.VMEM(distribution.shape, F32), in_...]
    reshape x1 -> x0, local copies, waits for them, and re-layouts: 1.52 us -> none  [frequency_weights(): return k.reshape(3 * NV, FREQ)]
    slice x5 -> x0, local copies, waits for them, and re-layouts: 1.28 us -> none  [frequency_weights(): other = jnp.roll(jnp.flip(k, (1, 2, 3)), 1, (1, 2, 3))]
    another operation x1 -> x0, other arithmetic: 1.2 us -> none  [frequency_weights(): k = jnp.stack(kernels)]
    pad x1 -> x0, local copies, waits for them, and re-layouts: 0.97 us -> none  [frequency_weights(): k = jnp.pad(k, ((0, 0), (0, 0), (0, 0), (0, NC - NV // 2 - 1)))]
    unnamed x11 -> x1, local copies, waits for them, and re-layouts: 0.95 us -> 0.93 us
where the time goes in v2:
time: 32.4 us; the launch traced here: 32.3 us
  Pallas kernels  31.4 us (97%)
  local copies, waits for them, and re-layouts  0.93 us (3%)
    pallas_call x1, Pallas kernels, per_device(): pl.pallas_call(kernel, out_shape=pltpu.VMEM(distribution.shape, F32), in_...  31.4 us
    unnamed x1, local copies, waits for them, and re-layouts  0.93 us

profile of v2, /device:TPU:1, one launch (start us, length us, event | category | flops | bytes accessed | tf_op | source)
XLA Modules:
  0.0 32.3 jit_solution(15996415993457011723)
XLA Ops:
  0.0 31.4 %shard_map.82 = f32[16,4,4,864]{3,2,1,0:T(4,128)S(1)} custom-call(f32[16,4,4,864]{3,2,1,0:T(4,128)} %dist.1, s32[4,4,16]{2,1,0:T(4,128)} %bitcast.7, f32[576,24]{1,0:T(8,128)} %bitcast.4, f32[576,24]{1,0:T(8,128)} %bitcast.5, f32[576,24]{1,0:T(8,128)} %bitcast.6, bf16[576,768]{1,0:T(8,128)(2,1)} %constant.6.clone.forward_hbm, ...), custom_call_target="tpu_custom_call" | custom-call | tf_op jit(solution)/shard_map/pallas_call | solution.py:342
  31.4 0.9 %copy.10 = f32[16,4,4,864]{3,2,1,0:T(4,128)} copy(f32[16,4,4,864]{3,2,1,0:T(4,128)S(1)} %shard_map.82) | data formatting | bytes 1769472

commit v3 on v2

--- a/solution.py
+++ b/solution.py
@@ -14,7 +14,7 @@
 NV, NC = 24, 16
 PLANE, HALF, LOCAL = NV * NV, NV * NV // 2, NV * NV * 3 // 2
 FREQ = NV * NC
-GROUPS, CELLS = 16, 8
+GROUPS, CHIPS, CELLS, TURNS = 16, 8, 4, 2
 ROWS = NV * CELLS
 SEGMENTS = ((0, 384), (512, 352), (256, 384))
 SEG = 384
@@ -30,16 +30,16 @@
     sine = np.round(np.sin(2 * np.pi * turns / NV), 12)
     forward = np.concatenate([cosine * keep, -sine * keep], 1)
     inverse = np.concatenate([(cosine * twice).T, (-sine * twice).T], 0)
-    turns = np.outer(np.arange(NV), np.arange(NV)) % NV
-    eye = np.eye(CELLS)
-    along_x = np.concatenate(
-        [
-            np.kron(np.round(np.cos(2 * np.pi * turns / NV), 12), eye),
-            np.kron(np.round(np.sin(2 * np.pi * turns / NV), 12), eye),
-        ],
-        0,
-    )
-    return tuple(jnp.asarray(t, dtype=BF16) for t in (forward, inverse, along_x))
+    row = np.arange(ROWS)
+    i_at, i_cell = 3 * (row // CELLS % CHIPS) + row // (CELLS * CHIPS), row % CELLS
+    a_at, a_cell = row % NV, row // NV
+    turns = np.outer(a_at, i_at) % NV
+    same = a_cell[:, None] == i_cell[None, :]
+    cosine = np.round(np.cos(2 * np.pi * turns / NV), 12) * same
+    sine = np.round(np.sin(2 * np.pi * turns / NV), 12) * same
+    into_x = np.concatenate([cosine, sine], 0)
+    from_x = np.concatenate([cosine.T, sine.T], 0)
+    return tuple(jnp.asarray(t, dtype=BF16) for t in (forward, inverse, into_x, from_x))
 
 
 def iota(shape, dim):
@@ -51,8 +51,8 @@
 
 
 def kernel(
-    dist, level_hbm, kernel_a, kernel_b, kernel_c, forward_hbm, inverse_hbm, along_hbm, out,
-    ext, face, halo, read, send, recv, field, packed, forward, inverse, along, raw, spread, sym, level,
+    dist, level_hbm, kernel_a, kernel_b, kernel_c, forward_hbm, inverse_hbm, into_hbm, from_hbm, out,
+    ext, face, halo, read, send, recv, back, packed, forward, inverse, into_x, from_x, raw, spread, sym, level,
     local_sem, table_sem, hop_sem, face_send, face_recv, send_sem, recv_sem, back_send, back_recv,
 ):
     me = lax.axis_index("vel")
@@ -81,7 +81,7 @@
         pltpu.make_async_copy(src, dst, table_sem.at[k])
         for k, (src, dst) in enumerate(
             (
-                (forward_hbm, forward), (inverse_hbm, inverse), (along_hbm, along),
+                (forward_hbm, forward), (inverse_hbm, inverse), (into_hbm, into_x), (from_hbm, from_x),
                 (kernel_a, raw.at[0:PLANE]), (kernel_b, raw.at[PLANE : 2 * PLANE]),
                 (kernel_c, raw.at[2 * PLANE : 3 * PLANE]),
             )
@@ -94,7 +94,11 @@
     beside = [x_low, x_high, y_low, y_high] + [{"vel": v} for v in near]
     for there in beside:
         pl.semaphore_signal(barrier, inc=1, device_id=there, device_id_type=MESH)
-    order = [8 + (k + 1) // 2 * (-1) ** k for k in range(GROUPS - 1)]
+    order = [(dz, t) for dz in (4, 3, -3, 2, -2, 1, -1, 0) for t in (0, 1) if (dz, t) != (0, 0)]
+
+    def partner(d):
+        return lax.rem((twin if d[1] else me) + 2 * d[0] + GROUPS, GROUPS)
+
 
     def remote(src, dst, send_at, recv_at, there):
         return pltpu.make_async_remote_copy(
@@ -185,55 +189,6 @@
     first_z, last_z = z_at == 0, z_at == 3
     step_x = jnp.where(falling, 1, -1)
 
-    for case in (True, False):
-
-        @pl.when(even == case)
-        def _():
-            for copy in y_copies(case):
-                copy.wait()
-
-    outer_halo = jnp.where(even, 5, 0)
-    for k, (first, width) in enumerate(SEGMENTS):
-        y = 5 - outer_halo if k == 2 else outer_halo
-        ext[1:9, y, :, first : first + width] = halo[k, :, 0:width].astype(F32).reshape(8, 8, width)
-
-    for case in (True, False):
-
-        @pl.when(falling == case)
-        def _():
-            x_copy(case).wait()
-
-    def plane(x, _):
-        for y in range(4):
-            f = ext[x + 1, y + 1]
-            flux = a_x * (f - ext[x + 1 + step_x, y + 1])
-            flux = flux + a_y * (f - jnp.where(up_y, ext[x + 1, y], ext[x + 1, y + 2]))
-            low = jnp.where(first_z, pltpu.roll(f, 5, 0), pltpu.roll(f, 1, 0))
-            high = jnp.where(last_z, pltpu.roll(f, 3, 0), pltpu.roll(f, 7, 0))
-            flux = flux + a_z * (f - jnp.where(up_z, low, high))
-            read[x, y] = f - flux
-        return 0
-
-    lax.fori_loop(0, 8, plane, 0)
-
-    chosen = dot(picker, read[...].reshape(256, LOCAL).astype(BF16))
-    send[...] = chosen.astype(BF16).reshape(GROUPS, CELLS, LOCAL)
-
-    def exchange(there, send_sems, recv_sems):
-        peer = lax.rem(me + there, GROUPS)
-        return remote(
-            send.at[peer], recv.at[me], send_sems.at[peer], recv_sems.at[me], {"vel": peer}
-        )
-
-    def arrived(d, recv_sems):
-        peer = lax.rem(me + d, GROUPS)
-        return remote(
-            send.at[peer], recv.at[peer], send_sem.at[peer], recv_sems.at[peer], {"vel": peer}
-        )
-
-    for d in order:
-        exchange(d, send_sem, recv_sem).start()
-    recv[me] = send[me]
     for load in table_loads:
         load.wait()
 
@@ -255,78 +210,152 @@
     )
     sym[...] = (both[: 3 * NV] + both[3 * NV :]) * (0.5 / float(NV**3))
 
-    for d in order:
-        arrived(d, recv_sem).wait_recv()
-
-    for p in range(GROUPS // 2):
-        left, right = recv[2 * p].astype(F32), recv[2 * p + 1].astype(F32)
-        at = 3 * p * CELLS
-        field[at : at + 8] = left[:, :PLANE]
-        field[at + 8 : at + 16, :HALF] = left[:, PLANE:]
-        field[at + 8 : at + 16, HALF:] = right[:, :HALF]
-        field[at + 16 : at + 24] = right[:, HALF:]
-
-    cells = field[...]
-    section = dot(cells.astype(BF16), forward[...]).astype(BF16)
-    turned = dot(along[...], section)
-    spec_re = turned[:ROWS, :FREQ] + turned[ROWS:, FREQ:]
-    spec_im = turned[:ROWS, FREQ:] - turned[ROWS:, :FREQ]
-    filtered = []
-    for k in range(3):
-        weights = jnp.broadcast_to(
-            sym[k * NV : (k + 1) * NV][:, None, :], (NV, CELLS, FREQ)
-        ).reshape(ROWS, FREQ)
-        weighted = jnp.concatenate([spec_re * weights, spec_im * weights], axis=1).astype(BF16)
-        turned = dot(along[...], weighted)
-        back = jnp.concatenate(
+    for case in (True, False):
+
+        @pl.when(even == case)
+        def _():
+            for copy in y_copies(case):
+                copy.wait()
+
+    outer_halo = jnp.where(even, 5, 0)
+    for k, (first, width) in enumerate(SEGMENTS):
+        y = 5 - outer_halo if k == 2 else outer_halo
+        ext[1:9, y, :, first : first + width] = halo[k, :, 0:width].astype(F32).reshape(8, 8, width)
+
+    for case in (True, False):
+
+        @pl.when(falling == case)
+        def _():
+            x_copy(case).wait()
+
+    def plane(x, _):
+        for y in range(4):
+            f = ext[x + 1, y + 1]
+            flux = a_x * (f - ext[x + 1 + step_x, y + 1])
+            flux = flux + a_y * (f - jnp.where(up_y, ext[x + 1, y], ext[x + 1, y + 2]))
+            low = jnp.where(first_z, pltpu.roll(f, 5, 0), pltpu.roll(f, 1, 0))
+            high = jnp.where(last_z, pltpu.roll(f, 3, 0), pltpu.roll(f, 7, 0))
+            flux = flux + a_z * (f - jnp.where(up_z, low, high))
+            read[x, y] = f - flux
+        return 0
+
+    lax.fori_loop(0, 8, plane, 0)
+
+    def block(ref, turn, device):
+        return ref.at[turn, device // 2, pl.ds(pl.multiple_of(CELLS * lax.rem(device, 2), CELLS), CELLS)]
+
+    def by_place(ref, turn, device):
+        chip = device // 2
+        rows = pl.ds(pl.multiple_of(CELLS * lax.rem(chip, 2), CELLS), CELLS)
+        return ref.at[turn, lax.rem(device, 2), chip // 2, rows]
+
+    def onward(turn, d):
+        there = partner(d)
+        return remote(
+            block(send, turn, there), by_place(recv, turn, me),
+            send_sem.at[turn, there], recv_sem.at[turn, me], {"vel": there},
+        )
+
+    def onward_from(turn, d):
+        there = partner(d)
+        return remote(
+            block(send, turn, there), by_place(recv, turn, there),
+            send_sem.at[turn, there], recv_sem.at[turn, there], {"vel": there},
+        )
+
+    def homeward(turn, d):
+        there = partner(d)
+        return remote(
+            by_place(back, turn, there), block(packed, turn, me),
+            back_send.at[turn, there], back_recv.at[turn, me], {"vel": there},
+        )
+
+    def homeward_from(turn, d):
+        there = partner(d)
+        return remote(
+            by_place(back, turn, there), block(packed, turn, there),
+            back_send.at[turn, there], back_recv.at[turn, there], {"vel": there},
+        )
+
+    values = read[...].reshape(256, LOCAL).astype(BF16)
+    for turn in range(TURNS):
+        chosen = dot(picker[64 * turn : 64 * turn + 64], values).astype(BF16)
+        send[turn] = chosen.reshape(GROUPS // 2, 2 * CELLS, LOCAL)
+        for d in order:
+            onward(turn, d).start()
+        own = pltpu.make_async_copy(
+            block(send, turn, me), by_place(recv, turn, me), send_sem.at[turn, me]
+        )
+        own.start()
+
+    for turn in range(TURNS):
+        pltpu.make_async_copy(
+            block(send, turn, me), by_place(recv, turn, me), send_sem.at[turn, me]
+        ).wait()
+        for d in order:
+            onward_from(turn, d).wait_recv()
+        left, right = (recv[turn, core].reshape(CHIPS * CELLS, LOCAL).astype(F32) for core in range(2))
+        cells = jnp.concatenate(
             [
-                turned[:ROWS, :FREQ] - turned[ROWS:, FREQ:],
-                turned[:ROWS, FREQ:] + turned[ROWS:, :FREQ],
+                left[:, :PLANE],
+                jnp.concatenate([left[:, PLANE:], right[:, :HALF]], axis=1),
+                right[:, HALF:],
             ],
-            axis=1,
-        ).astype(BF16)
-        filtered.append(dot(back, inverse[...]))
-    field[...] = filtered[0] * filtered[1] - cells * filtered[2]
-
-    for d in order:
-        peer = lax.rem(me + d, GROUPS)
-        exchange(d, send_sem, recv_sem).wait_send()
-    for p in range(GROUPS // 2):
-        at = 3 * p * CELLS
-        send[2 * p] = jnp.concatenate(
-            [field[at : at + 8], field[at + 8 : at + 16, :HALF]], axis=1
-        ).astype(BF16)
-        send[2 * p + 1] = jnp.concatenate(
-            [field[at + 8 : at + 16, HALF:], field[at + 16 : at + 24]], axis=1
-        ).astype(BF16)
-
-    def give_back(d):
-        peer = lax.rem(me + d, GROUPS)
-        return remote(
-            send.at[peer], packed.at[me], back_send.at[peer], back_recv.at[me], {"vel": peer}
-        )
-
-    def came_back(d):
-        peer = lax.rem(me + d, GROUPS)
-        return remote(
-            send.at[peer], packed.at[peer], back_send.at[peer], back_recv.at[peer], {"vel": peer}
-        )
-
-    for d in order:
-        give_back(d).start()
-    packed[me] = send[me]
-    for d in order:
-        came_back(d).wait_recv()
+            axis=0,
+        )
+        section = dot(cells.astype(BF16), forward[...]).astype(BF16)
+        turned = dot(into_x[...], section)
+        spec_re = turned[:ROWS, :FREQ] + turned[ROWS:, FREQ:]
+        spec_im = turned[:ROWS, FREQ:] - turned[ROWS:, :FREQ]
+        spectra = []
+        for k in range(3):
+            weights = sym[k * NV : (k + 1) * NV]
+            weights = jnp.concatenate([weights] * CELLS, axis=0)
+            weighted = jnp.concatenate([spec_re * weights, spec_im * weights], axis=1).astype(BF16)
+            turned = dot(from_x[...], weighted)
+            spectra.append(
+                jnp.concatenate(
+                    [
+                        turned[:ROWS, :FREQ] - turned[ROWS:, FREQ:],
+                        turned[:ROWS, FREQ:] + turned[ROWS:, :FREQ],
+                    ],
+                    axis=1,
+                ).astype(BF16)
+            )
+        filtered = dot(jnp.concatenate(spectra, axis=0), inverse[...])
+        terms = filtered[:ROWS] * filtered[ROWS : 2 * ROWS] - cells * filtered[2 * ROWS :]
+        third = CHIPS * CELLS
+        low, middle, high = (terms[third * q : third * q + third] for q in range(3))
+        back[turn, 0] = jnp.concatenate([low, middle[:, :HALF]], axis=1).astype(BF16).reshape(
+            CHIPS // 2, 2 * CELLS, LOCAL
+        )
+        back[turn, 1] = jnp.concatenate([middle[:, HALF:], high], axis=1).astype(BF16).reshape(
+            CHIPS // 2, 2 * CELLS, LOCAL
+        )
+        for d in order:
+            homeward(turn, d).start()
+        pltpu.make_async_copy(
+            by_place(back, turn, me), block(packed, turn, me), back_send.at[turn, me]
+        ).start()
+
+    for turn in range(TURNS):
+        pltpu.make_async_copy(
+            by_place(back, turn, me), block(packed, turn, me), back_send.at[turn, me]
+        ).wait()
+        for d in order:
+            homeward_from(turn, d).wait_recv()
 
     rates = lax.dot_general(
-        placer, packed[...].reshape(GROUPS * CELLS, LOCAL), (((0,), (0,)), ((), ())),
+        placer, packed[...].reshape(TURNS * GROUPS * CELLS, LOCAL), (((0,), (0,)), ((), ())),
         preferred_element_type=F32,
     )
     evolved = read[...] + rates.reshape(8, 4, 8, LOCAL)
     for part in range(2):
         out[8 * part : 8 * part + 8] = evolved[:, :, 4 * part : 4 * part + 4]
-    for d in order:
-        give_back(d).wait_send()
+    for turn in range(TURNS):
+        for d in order:
+            onward(turn, d).wait_send()
+            homeward(turn, d).wait_send()
 
 
 def in_hbm(array):
@@ -334,7 +363,7 @@
 
 
 def per_device(distribution, refine_level, gain_one, gain_two, loss_kernel):
-    forward, inverse, along = tables()
+    constants = tables()
     kernels = [k.reshape(PLANE, NV) for k in (gain_one, gain_two, loss_kernel)]
     hbm = pl.BlockSpec(memory_space=pltpu.MemorySpace.HBM)
     vmem = pl.BlockSpec(memory_space=pltpu.VMEM)
@@ -342,31 +371,32 @@
     return pl.pallas_call(
         kernel,
         out_shape=pltpu.VMEM(distribution.shape, F32),
-        in_specs=[hbm] * 8,
+        in_specs=[hbm] * 9,
         out_specs=vmem,
         scratch_shapes=[
             pltpu.VMEM((10, 6, 8, LOCAL), F32),
             pltpu.VMEM((3, 64, SEG), BF16),
             pltpu.VMEM((3, 64, SEG), BF16),
             pltpu.VMEM((8, 4, 8, LOCAL), F32),
-            pltpu.VMEM((GROUPS, CELLS, LOCAL), BF16),
-            pltpu.VMEM((GROUPS, CELLS, LOCAL), BF16),
-            pltpu.VMEM((ROWS, PLANE), F32),
-            pltpu.VMEM((GROUPS, CELLS, LOCAL), BF16),
+            pltpu.VMEM((TURNS, GROUPS // 2, 2 * CELLS, LOCAL), BF16),
+            pltpu.VMEM((TURNS, 2, CHIPS // 2, 2 * CELLS, LOCAL), BF16),
+            pltpu.VMEM((TURNS, 2, CHIPS // 2, 2 * CELLS, LOCAL), BF16),
+            pltpu.VMEM((TURNS, GROUPS // 2, 2 * CELLS, LOCAL), BF16),
             pltpu.VMEM((PLANE, 2 * FREQ), BF16),
             pltpu.VMEM((2 * FREQ, PLANE), BF16),
+            pltpu.VMEM((2 * ROWS, ROWS), BF16),
             pltpu.VMEM((2 * ROWS, ROWS), BF16),
             pltpu.VMEM((3 * PLANE, NV), F32),
             pltpu.VMEM((3 * NV, PLANE), F32),
             pltpu.VMEM((3 * NV, FREQ), F32),
             pltpu.VMEM((4, 4, 16), jnp.int32),
-            dma((11,)), dma((6,)), pltpu.SemaphoreType.REGULAR((6,)), dma((3,)), dma((3,)),
-            dma((GROUPS,)), dma((GROUPS,)), dma((GROUPS,)), dma((GROUPS,)),
+            dma((11,)), dma((7,)), pltpu.SemaphoreType.REGULAR((6,)), dma((3,)), dma((3,)),
+            *[dma((TURNS, GROUPS))] * 4,
         ],
         compiler_params=pltpu.CompilerParams(
             collective_id=0, has_side_effects=True, vmem_limit_bytes=48 << 20
         ),
-    )(*map(in_hbm, (distribution, refine_level.transpose(1, 2, 0), *kernels, forward, inverse, along)))
+    )(*map(in_hbm, (distribution, refine_level.transpose(1, 2, 0), *kernels, *constants)))
 
 
 def solution(mesh):

time: 32.4 us -> 32.1 us (level)
  no operation moved by 1% of the time
where the time goes in v3:
time: 32.1 us; the launch traced here: 32 us
  Pallas kernels  31.1 us (97%)
  local copies, waits for them, and re-layouts  0.93 us (3%)
    pallas_call x1, Pallas kernels, per_device(): pl.pallas_call(kernel, out_shape=pltpu.VMEM(distribution.shape, F32), in_...  31.1 us
    unnamed x1, local copies, waits for them, and re-layouts  0.93 us

profile of v3, /device:TPU:1, one launch (start us, length us, event | category | flops | bytes accessed | tf_op | source)
XLA Modules:
  0.0 32.0 jit_solution(10505351308401526289)
XLA Ops:
  0.0 31.1 %shard_map.91 = f32[16,4,4,864]{3,2,1,0:T(4,128)S(1)} custom-call(f32[16,4,4,864]{3,2,1,0:T(4,128)} %dist.1, s32[4,4,16]{2,1,0:T(4,128)} %bitcast.7, f32[576,24]{1,0:T(8,128)} %bitcast.4, f32[576,24]{1,0:T(8,128)} %bitcast.5, f32[576,24]{1,0:T(8,128)} %bitcast.6, bf16[576,768]{1,0:T(8,128)(2,1)} %constant.8.clone.forward_hbm, ...), custom_call_target="tpu_custom_call" | custom-call | tf_op jit(solution)/shard_map/pallas_call | solution.py:371
  31.1 0.9 %copy.11 = f32[16,4,4,864]{3,2,1,0:T(4,128)} copy(f32[16,4,4,864]{3,2,1,0:T(4,128)S(1)} %shard_map.91) | data formatting | bytes 1769472

commit v4 on v3

--- a/solution.py
+++ b/solution.py
@@ -18,6 +18,7 @@
 ROWS = NV * CELLS
 SEGMENTS = ((0, 384), (512, 352), (256, 384))
 SEG = 384
+Y_ORDER = (1, 2, 0, 3)
 
 
 def tables():
@@ -52,7 +53,7 @@
 
 def kernel(
     dist, level_hbm, kernel_a, kernel_b, kernel_c, forward_hbm, inverse_hbm, into_hbm, from_hbm, out,
-    ext, face, halo, read, send, recv, back, packed, forward, inverse, into_x, from_x, raw, spread, sym, level,
+    ext, face, halo, edge_out, edge_in, read, values, send, recv, back, packed, forward, inverse, into_x, from_x, raw, spread, sym, level,
     local_sem, table_sem, hop_sem, face_send, face_recv, send_sem, recv_sem, back_send, back_recv,
 ):
     me = lax.axis_index("vel")
@@ -107,11 +108,7 @@
         )
 
     def x_copy(up):
-        if up:
-            return remote(
-                dist.at[0], ext.at[9, 1:5, 4:8], face_send.at[0], face_recv.at[0], x_low
-            )
-        return remote(dist.at[15], ext.at[0, 1:5, 0:4], face_send.at[0], face_recv.at[0], x_high)
+        return remote(edge_out, edge_in, face_send.at[0], face_recv.at[0], x_low if up else x_high)
 
     def y_copies(is_even):
         outer = remote(
@@ -131,6 +128,11 @@
         y = 5 - outer_y if k == 2 else outer_y
         face[k, :, 0:width] = ext[1:9, y, :, first : first + width].reshape(64, width).astype(BF16)
 
+    for load in loads[4:]:
+        load.wait()
+    edge = jnp.where(falling, ext[1, 1:5, 0:4], ext[8, 1:5, 4:8])
+    edge_out[...] = edge.reshape(16, LOCAL).astype(BF16)
+
     pl.semaphore_wait(barrier, len(beside))
     for case in (True, False):
 
@@ -147,22 +149,25 @@
 
     for load in table_loads:
         load.start()
-    for k in range(3):
+    def tell(k):
         for side, d in enumerate((2, GROUPS - 2)):
             pl.semaphore_signal(
                 hop_sem.at[2 * k + side], inc=1, device_id={"vel": lax.rem(me + d, GROUPS)},
                 device_id_type=MESH,
             )
+
+    def hear(k):
         for side in range(2):
             pl.semaphore_wait(hop_sem.at[2 * k + side], 1)
 
-    for load in loads[4:]:
-        load.wait()
+    tell(0)
+
     levels = jnp.concatenate([level[y] for y in range(4)], axis=0).astype(F32).astype(BF16)
     r = iota((16, 256), 1)
     row = iota((16, 256), 0)
     x_hot = (row == lax.rem(r // 4, 2) * 8 + r // 32).astype(F32).astype(BF16)
-    yz_hot = row == lax.rem(r // 8, 4) * 4 + lax.rem(r, 4)
+    y_rank = lax.rem(r // 8, 4)
+    yz_hot = row == jnp.where(y_rank < 2, y_rank + 1, 3 * y_rank - 6) * 4 + lax.rem(r, 4)
     by_yz = dot(levels, x_hot)
     level_row = jnp.sum(jnp.where(yz_hot, by_yz, 0.0), axis=0, keepdims=True)
     active = (level_row > 0.5).astype(F32)
@@ -188,6 +193,110 @@
     z_at = lax.rem(iota(shape, 0), 4)
     first_z, last_z = z_at == 0, z_at == 3
     step_x = jnp.where(falling, 1, -1)
+
+    def rows(x, pair):
+        done = []
+        for rank in (2 * pair, 2 * pair + 1):
+            y = Y_ORDER[rank]
+            f = ext[x + 1, y + 1]
+            flux = a_x * (f - ext[x + 1 + step_x, y + 1])
+            flux = flux + a_y * (f - jnp.where(up_y, ext[x + 1, y], ext[x + 1, y + 2]))
+            low = jnp.where(first_z, pltpu.roll(f, 5, 0), pltpu.roll(f, 1, 0))
+            high = jnp.where(last_z, pltpu.roll(f, 3, 0), pltpu.roll(f, 7, 0))
+            flux = flux + a_z * (f - jnp.where(up_z, low, high))
+            read[x, rank] = f - flux
+            done.append(f - flux)
+        at = pl.multiple_of(32 * x + 16 * pair, 16)
+        values[pl.ds(at, 16), :] = jnp.concatenate(done, axis=0).astype(BF16)
+
+    hear(0)
+    tell(1)
+    first_inner = jnp.where(falling, 0, 1)
+
+    def inner(k, _):
+        rows(first_inner + k, 0)
+        return 0
+
+    lax.fori_loop(0, 7, inner, 0)
+    hear(1)
+    tell(2)
+
+    for case in (True, False):
+
+        @pl.when(even == case)
+        def _():
+            for copy in y_copies(case):
+                copy.wait()
+
+    outer_halo = jnp.where(even, 5, 0)
+    for k, (first, width) in enumerate(SEGMENTS):
+        y = 5 - outer_halo if k == 2 else outer_halo
+        ext[1:9, y, :, first : first + width] = halo[k, :, 0:width].astype(F32).reshape(8, 8, width)
+
+    for case in (True, False):
+
+        @pl.when(falling == case)
+        def _():
+            x_copy(case).wait()
+
+    edge = edge_in[...].astype(F32).reshape(4, 4, LOCAL)
+    ext[9, 1:5, 4:8] = edge
+    ext[0, 1:5, 0:4] = edge
+
+    rows(jnp.where(falling, 7, 0), 0)
+
+    def outer(x, _):
+        rows(x, 1)
+        return 0
+
+    lax.fori_loop(0, 8, outer, 0)
+    def block(ref, turn, device):
+        return ref.at[turn, device // 2, pl.ds(pl.multiple_of(CELLS * lax.rem(device, 2), CELLS), CELLS)]
+
+    def by_place(ref, turn, device):
+        chip = device // 2
+        rows = pl.ds(pl.multiple_of(CELLS * lax.rem(chip, 2), CELLS), CELLS)
+        return ref.at[turn, lax.rem(device, 2), chip // 2, rows]
+
+    def onward(turn, d):
+        there = partner(d)
+        return remote(
+            block(send, turn, there), by_place(recv, turn, me),
+            send_sem.at[turn, there], recv_sem.at[turn, me], {"vel": there},
+        )
+
+    def onward_from(turn, d):
+        there = partner(d)
+        return remote(
+            block(send, turn, there), by_place(recv, turn, there),
+            send_sem.at[turn, there], recv_sem.at[turn, there], {"vel": there},
+        )
+
+    def homeward(turn, d):
+        there = partner(d)
+        return remote(
+            by_place(back, turn, there), block(packed, turn, me),
+            back_send.at[turn, there], back_recv.at[turn, me], {"vel": there},
+        )
+
+    def homeward_from(turn, d):
+        there = partner(d)
+        return remote(
+            by_place(back, turn, there), block(packed, turn, there),
+            back_send.at[turn, there], back_recv.at[turn, there], {"vel": there},
+        )
+
+    for turn in range(TURNS):
+        chosen = dot(picker[64 * turn : 64 * turn + 64], values[...]).astype(BF16)
+        send[turn] = chosen.reshape(GROUPS // 2, 2 * CELLS, LOCAL)
+        if turn == 0:
+            hear(2)
+        for d in order:
+            onward(turn, d).start()
+        own = pltpu.make_async_copy(
+            block(send, turn, me), by_place(recv, turn, me), send_sem.at[turn, me]
+        )
+        own.start()
 
     for load in table_loads:
         load.wait()
@@ -209,84 +318,6 @@
         turned, (pick == other).astype(F32).astype(BF16)
     )
     sym[...] = (both[: 3 * NV] + both[3 * NV :]) * (0.5 / float(NV**3))
-
-    for case in (True, False):
-
-        @pl.when(even == case)
-        def _():
-            for copy in y_copies(case):
-                copy.wait()
-
-    outer_halo = jnp.where(even, 5, 0)
-    for k, (first, width) in enumerate(SEGMENTS):
-        y = 5 - outer_halo if k == 2 else outer_halo
-        ext[1:9, y, :, first : first + width] = halo[k, :, 0:width].astype(F32).reshape(8, 8, width)
-
-    for case in (True, False):
-
-        @pl.when(falling == case)
-        def _():
-            x_copy(case).wait()
-
-    def plane(x, _):
-        for y in range(4):
-            f = ext[x + 1, y + 1]
-            flux = a_x * (f - ext[x + 1 + step_x, y + 1])
-            flux = flux + a_y * (f - jnp.where(up_y, ext[x + 1, y], ext[x + 1, y + 2]))
-            low = jnp.where(first_z, pltpu.roll(f, 5, 0), pltpu.roll(f, 1, 0))
-            high = jnp.where(last_z, pltpu.roll(f, 3, 0), pltpu.roll(f, 7, 0))
-            flux = flux + a_z * (f - jnp.where(up_z, low, high))
-            read[x, y] = f - flux
-        return 0
-
-    lax.fori_loop(0, 8, plane, 0)
-
-    def block(ref, turn, device):
-        return ref.at[turn, device // 2, pl.ds(pl.multiple_of(CELLS * lax.rem(device, 2), CELLS), CELLS)]
-
-    def by_place(ref, turn, device):
-        chip = device // 2
-        rows = pl.ds(pl.multiple_of(CELLS * lax.rem(chip, 2), CELLS), CELLS)
-        return ref.at[turn, lax.rem(device, 2), chip // 2, rows]
-
-    def onward(turn, d):
-        there = partner(d)
-        return remote(
-            block(send, turn, there), by_place(recv, turn, me),
-            send_sem.at[turn, there], recv_sem.at[turn, me], {"vel": there},
-        )
-
-    def onward_from(turn, d):
-        there = partner(d)
-        return remote(
-            block(send, turn, there), by_place(recv, turn, there),
-            send_sem.at[turn, there], recv_sem.at[turn, there], {"vel": there},
-        )
-
-    def homeward(turn, d):
-        there = partner(d)
-        return remote(
-            by_place(back, turn, there), block(packed, turn, me),
-            back_send.at[turn, there], back_recv.at[turn, me], {"vel": there},
-        )
-
-    def homeward_from(turn, d):
-        there = partner(d)
-        return remote(
-            by_place(back, turn, there), block(packed, turn, there),
-            back_send.at[turn, there], back_recv.at[turn, there], {"vel": there},
-        )
-
-    values = read[...].reshape(256, LOCAL).astype(BF16)
-    for turn in range(TURNS):
-        chosen = dot(picker[64 * turn : 64 * turn + 64], values).astype(BF16)
-        send[turn] = chosen.reshape(GROUPS // 2, 2 * CELLS, LOCAL)
-        for d in order:
-            onward(turn, d).start()
-        own = pltpu.make_async_copy(
-            block(send, turn, me), by_place(recv, turn, me), send_sem.at[turn, me]
-        )
-        own.start()
 
     for turn in range(TURNS):
         pltpu.make_async_copy(
@@ -351,7 +382,8 @@
     )
     evolved = read[...] + rates.reshape(8, 4, 8, LOCAL)
     for part in range(2):
-        out[8 * part : 8 * part + 8] = evolved[:, :, 4 * part : 4 * part + 4]
+        for rank, y in enumerate(Y_ORDER):
+            out[8 * part : 8 * part + 8, y] = evolved[:, rank, 4 * part : 4 * part + 4]
     for turn in range(TURNS):
         for d in order:
             onward(turn, d).wait_send()
@@ -377,7 +409,10 @@
             pltpu.VMEM((10, 6, 8, LOCAL), F32),
             pltpu.VMEM((3, 64, SEG), BF16),
             pltpu.VMEM((3, 64, SEG), BF16),
+            pltpu.VMEM((16, LOCAL), BF16),
+            pltpu.VMEM((16, LOCAL), BF16),
             pltpu.VMEM((8, 4, 8, LOCAL), F32),
+            pltpu.VMEM((256, LOCAL), BF16),
             pltpu.VMEM((TURNS, GROUPS // 2, 2 * CELLS, LOCAL), BF16),
             pltpu.VMEM((TURNS, 2, CHIPS // 2, 2 * CELLS, LOCAL), BF16),
             pltpu.VMEM((TURNS, 2, CHIPS // 2, 2 * CELLS, LOCAL), BF16),

time: 32.1 us -> 30.7 us (0.956)
  Pallas kernels: 31.1 us -> 29.7 us
    pallas_call x1, Pallas kernels: 31.1 us -> 29.7 us  [per_device(): pl.pallas_call(kernel, out_shape=pltpu.VMEM(distribution.shape, F32), in_...]
where the time goes in v4:
time: 30.7 us; the launch traced here: 30.6 us
  Pallas kernels  29.7 us (97%)
  local copies, waits for them, and re-layouts  0.93 us (3%)
    pallas_call x1, Pallas kernels, per_device(): pl.pallas_call(kernel, out_shape=pltpu.VMEM(distribution.shape, F32), in_...  29.7 us
    unnamed x1, local copies, waits for them, and re-layouts  0.93 us

profile of v4, /device:TPU:1, one launch (start us, length us, event | category | flops | bytes accessed | tf_op | source)
XLA Modules:
  0.0 30.6 jit_solution(4031243581433617128)
XLA Ops:
  0.0 29.7 %shard_map.91 = f32[16,4,4,864]{3,2,1,0:T(4,128)S(1)} custom-call(f32[16,4,4,864]{3,2,1,0:T(4,128)} %dist.1, s32[4,4,16]{2,1,0:T(4,128)} %bitcast.7, f32[576,24]{1,0:T(8,128)} %bitcast.4, f32[576,24]{1,0:T(8,128)} %bitcast.5, f32[576,24]{1,0:T(8,128)} %bitcast.6, bf16[576,768]{1,0:T(8,128)(2,1)} %constant.8.clone.forward_hbm, ...), custom_call_target="tpu_custom_call" | custom-call | tf_op jit(solution)/shard_map/pallas_call | solution.py:403
  29.7 0.9 %copy.11 = f32[16,4,4,864]{3,2,1,0:T(4,128)} copy(f32[16,4,4,864]{3,2,1,0:T(4,128)S(1)} %shard_map.91) | data formatting | bytes 1769472

commit v5 on v4

--- a/solution.py
+++ b/solution.py
@@ -64,6 +64,12 @@
     falling = me < GROUPS // 2
     even = lax.rem(me, 2) == 0
 
+    barrier = pltpu.get_barrier_semaphore()
+    twin = me + 1 - 2 * lax.rem(me, 2)
+    near = [twin] + [lax.rem(m + d, GROUPS) for m in (me, twin) for d in (2, GROUPS - 2)]
+    beside = [x_low, x_high, y_low, y_high] + [{"vel": v} for v in near]
+    for there in beside:
+        pl.semaphore_signal(barrier, inc=1, device_id=there, device_id_type=MESH)
     loads = [
         pltpu.make_async_copy(
             dist.at[8 * s : 8 * s + 8, y], ext.at[1:9, y + 1, 4 * s : 4 * s + 4], local_sem.at[2 * y + s]
@@ -89,12 +95,6 @@
         )
     ]
 
-    barrier = pltpu.get_barrier_semaphore()
-    twin = me + 1 - 2 * lax.rem(me, 2)
-    near = [twin] + [lax.rem(m + d, GROUPS) for m in (me, twin) for d in (2, GROUPS - 2)]
-    beside = [x_low, x_high, y_low, y_high] + [{"vel": v} for v in near]
-    for there in beside:
-        pl.semaphore_signal(barrier, inc=1, device_id=there, device_id_type=MESH)
     order = [(dz, t) for dz in (4, 3, -3, 2, -2, 1, -1, 0) for t in (0, 1) if (dz, t) != (0, 0)]
 
     def partner(d):
@@ -250,53 +250,39 @@
         return 0
 
     lax.fori_loop(0, 8, outer, 0)
-    def block(ref, turn, device):
-        return ref.at[turn, device // 2, pl.ds(pl.multiple_of(CELLS * lax.rem(device, 2), CELLS), CELLS)]
-
     def by_place(ref, turn, device):
-        chip = device // 2
-        rows = pl.ds(pl.multiple_of(CELLS * lax.rem(chip, 2), CELLS), CELLS)
-        return ref.at[turn, lax.rem(device, 2), chip // 2, rows]
+        return ref.at[turn, lax.rem(device, 2), device // 2]
 
     def onward(turn, d):
         there = partner(d)
         return remote(
-            block(send, turn, there), by_place(recv, turn, me),
-            send_sem.at[turn, there], recv_sem.at[turn, me], {"vel": there},
-        )
-
-    def onward_from(turn, d):
-        there = partner(d)
-        return remote(
-            block(send, turn, there), by_place(recv, turn, there),
-            send_sem.at[turn, there], recv_sem.at[turn, there], {"vel": there},
+            send.at[turn, there], by_place(recv, turn, me), send_sem.at[turn], recv_sem.at[turn],
+            {"vel": there},
         )
 
     def homeward(turn, d):
         there = partner(d)
         return remote(
-            by_place(back, turn, there), block(packed, turn, me),
-            back_send.at[turn, there], back_recv.at[turn, me], {"vel": there},
-        )
-
-    def homeward_from(turn, d):
-        there = partner(d)
-        return remote(
-            by_place(back, turn, there), block(packed, turn, there),
-            back_send.at[turn, there], back_recv.at[turn, there], {"vel": there},
-        )
+            by_place(back, turn, there), packed.at[turn, me], back_send.at[turn], back_recv.at[turn],
+            {"vel": there},
+        )
+
+    def all_of(ref, turn, sem):
+        pltpu.make_async_copy(ref.at[turn], ref.at[turn], sem.at[turn]).wait()
+
+    def others_of(ref, turn, sem):
+        pltpu.make_async_copy(
+            ref.at[turn, 0 : GROUPS - 1], ref.at[turn, 0 : GROUPS - 1], sem.at[turn]
+        ).wait()
 
     for turn in range(TURNS):
-        chosen = dot(picker[64 * turn : 64 * turn + 64], values[...]).astype(BF16)
-        send[turn] = chosen.reshape(GROUPS // 2, 2 * CELLS, LOCAL)
+        chosen = dot(picker[64 * turn : 64 * turn + 64], values[...])
+        send[turn] = chosen.reshape(GROUPS, CELLS, LOCAL).astype(BF16)
         if turn == 0:
             hear(2)
         for d in order:
             onward(turn, d).start()
-        own = pltpu.make_async_copy(
-            block(send, turn, me), by_place(recv, turn, me), send_sem.at[turn, me]
-        )
-        own.start()
+        pltpu.make_async_copy(send.at[turn, me], by_place(recv, turn, me), recv_sem.at[turn]).start()
 
     for load in table_loads:
         load.wait()
@@ -320,12 +306,10 @@
     sym[...] = (both[: 3 * NV] + both[3 * NV :]) * (0.5 / float(NV**3))
 
     for turn in range(TURNS):
-        pltpu.make_async_copy(
-            block(send, turn, me), by_place(recv, turn, me), send_sem.at[turn, me]
-        ).wait()
-        for d in order:
-            onward_from(turn, d).wait_recv()
-        left, right = (recv[turn, core].reshape(CHIPS * CELLS, LOCAL).astype(F32) for core in range(2))
+        all_of(recv, turn, recv_sem)
+        left, right = (
+            recv[turn, core].astype(F32).reshape(CHIPS * CELLS, LOCAL) for core in range(2)
+        )
         cells = jnp.concatenate(
             [
                 left[:, :PLANE],
@@ -357,37 +341,34 @@
         terms = filtered[:ROWS] * filtered[ROWS : 2 * ROWS] - cells * filtered[2 * ROWS :]
         third = CHIPS * CELLS
         low, middle, high = (terms[third * q : third * q + third] for q in range(3))
-        back[turn, 0] = jnp.concatenate([low, middle[:, :HALF]], axis=1).astype(BF16).reshape(
-            CHIPS // 2, 2 * CELLS, LOCAL
-        )
-        back[turn, 1] = jnp.concatenate([middle[:, HALF:], high], axis=1).astype(BF16).reshape(
-            CHIPS // 2, 2 * CELLS, LOCAL
-        )
+        sides = (
+            jnp.concatenate([low, middle[:, :HALF]], axis=1),
+            jnp.concatenate([middle[:, HALF:], high], axis=1),
+        )
+        for core in range(2):
+            back[turn, core] = sides[core].reshape(CHIPS, CELLS, LOCAL).astype(BF16)
         for d in order:
             homeward(turn, d).start()
         pltpu.make_async_copy(
-            by_place(back, turn, me), block(packed, turn, me), back_send.at[turn, me]
+            by_place(back, turn, me), packed.at[turn, me], back_recv.at[turn]
         ).start()
 
     for turn in range(TURNS):
-        pltpu.make_async_copy(
-            by_place(back, turn, me), block(packed, turn, me), back_send.at[turn, me]
-        ).wait()
-        for d in order:
-            homeward_from(turn, d).wait_recv()
-
-    rates = lax.dot_general(
-        placer, packed[...].reshape(TURNS * GROUPS * CELLS, LOCAL), (((0,), (0,)), ((), ())),
-        preferred_element_type=F32,
-    )
-    evolved = read[...] + rates.reshape(8, 4, 8, LOCAL)
+        all_of(packed, turn, back_recv)
+        rates = lax.dot_general(
+            placer[64 * turn : 64 * turn + 64],
+            packed[turn].astype(F32).reshape(GROUPS * CELLS, LOCAL).astype(BF16),
+            (((0,), (0,)), ((), ())), preferred_element_type=F32,
+        )
+        evolved = read[...] + rates.reshape(8, 4, 8, LOCAL)
+        if turn < TURNS - 1:
+            read[...] = evolved
     for part in range(2):
         for rank, y in enumerate(Y_ORDER):
             out[8 * part : 8 * part + 8, y] = evolved[:, rank, 4 * part : 4 * part + 4]
     for turn in range(TURNS):
-        for d in order:
-            onward(turn, d).wait_send()
-            homeward(turn, d).wait_send()
+        others_of(send, turn, send_sem)
+        others_of(packed, turn, back_send)
 
 
 def in_hbm(array):
@@ -413,10 +394,10 @@
             pltpu.VMEM((16, LOCAL), BF16),
             pltpu.VMEM((8, 4, 8, LOCAL), F32),
             pltpu.VMEM((256, LOCAL), BF16),
-            pltpu.VMEM((TURNS, GROUPS // 2, 2 * CELLS, LOCAL), BF16),
-            pltpu.VMEM((TURNS, 2, CHIPS // 2, 2 * CELLS, LOCAL), BF16),
-            pltpu.VMEM((TURNS, 2, CHIPS // 2, 2 * CELLS, LOCAL), BF16),
-            pltpu.VMEM((TURNS, GROUPS // 2, 2 * CELLS, LOCAL), BF16),
+            pltpu.VMEM((TURNS, GROUPS, CELLS, LOCAL), BF16),
+            pltpu.VMEM((TURNS, 2, CHIPS, CELLS, LOCAL), BF16),
+            pltpu.VMEM((TURNS, 2, CHIPS, CELLS, LOCAL), BF16),
+            pltpu.VMEM((TURNS, GROUPS, CELLS, LOCAL), BF16),
             pltpu.VMEM((PLANE, 2 * FREQ), BF16),
             pltpu.VMEM((2 * FREQ, PLANE), BF16),
             pltpu.VMEM((2 * ROWS, ROWS), BF16),
@@ -426,7 +407,7 @@
             pltpu.VMEM((3 * NV, FREQ), F32),
             pltpu.VMEM((4, 4, 16), jnp.int32),
             dma((11,)), dma((7,)), pltpu.SemaphoreType.REGULAR((6,)), dma((3,)), dma((3,)),
-            *[dma((TURNS, GROUPS))] * 4,
+            *[dma((TURNS,))] * 4,
         ],
         compiler_params=pltpu.CompilerParams(
             collective_id=0, has_side_effects=True, vmem_limit_bytes=48 << 20

time: 30.7 us -> 29.5 us (0.961)
  Pallas kernels: 29.7 us -> 28.5 us
    pallas_call x1, Pallas kernels: 29.7 us -> 28.5 us  [per_device(): pl.pallas_call(kernel, out_shape=pltpu.VMEM(distribution.shape, F32), in_...]
where the time goes in v5:
time: 29.5 us; the launch traced here: 29.4 us
  Pallas kernels  28.5 us (97%)
  local copies, waits for them, and re-layouts  0.93 us (3%)
    pallas_call x1, Pallas kernels, per_device(): pl.pallas_call(kernel, out_shape=pltpu.VMEM(distribution.shape, F32), in_...  28.5 us
    unnamed x1, local copies, waits for them, and re-layouts  0.93 us

profile of v5, /device:TPU:1, one launch (start us, length us, event | category | flops | bytes accessed | tf_op | source)
XLA Modules:
  0.0 29.4 jit_solution(17259609479900229333)
XLA Ops:
  0.0 28.5 %shard_map.91 = f32[16,4,4,864]{3,2,1,0:T(4,128)S(1)} custom-call(f32[16,4,4,864]{3,2,1,0:T(4,128)} %dist.1, s32[4,4,16]{2,1,0:T(4,128)} %bitcast.7, f32[576,24]{1,0:T(8,128)} %bitcast.4, f32[576,24]{1,0:T(8,128)} %bitcast.5, f32[576,24]{1,0:T(8,128)} %bitcast.6, bf16[576,768]{1,0:T(8,128)(2,1)} %constant.8.clone.forward_hbm, ...), custom_call_target="tpu_custom_call" | custom-call | tf_op jit(solution)/shard_map/pallas_call | solution.py:384
  28.5 0.9 %copy.11 = f32[16,4,4,864]{3,2,1,0:T(4,128)} copy(f32[16,4,4,864]{3,2,1,0:T(4,128)S(1)} %shard_map.91) | data formatting | bytes 1769472

commit v6 on v5

--- a/solution.py
+++ b/solution.py
@@ -14,7 +14,8 @@
 NV, NC = 24, 16
 PLANE, HALF, LOCAL = NV * NV, NV * NV // 2, NV * NV * 3 // 2
 FREQ = NV * NC
-GROUPS, CHIPS, CELLS, TURNS = 16, 8, 4, 2
+GROUPS, CHIPS, CELLS, TURNS = 16, 8, 2, 4
+SLOTS = GROUPS * CELLS
 ROWS = NV * CELLS
 SEGMENTS = ((0, 384), (512, 352), (256, 384))
 SEG = 384
@@ -72,15 +73,14 @@
         pl.semaphore_signal(barrier, inc=1, device_id=there, device_id_type=MESH)
     loads = [
         pltpu.make_async_copy(
-            dist.at[8 * s : 8 * s + 8, y], ext.at[1:9, y + 1, 4 * s : 4 * s + 4], local_sem.at[2 * y + s]
-        )
-        for y in (0, 3, 1, 2)
+            dist.at[8 * s : 8 * s + 8], ext.at[1:9, 1:5, 4 * s : 4 * s + 4], local_sem.at[s]
+        )
         for s in range(2)
     ]
     loads += [
-        pltpu.make_async_copy(dist.at[8], ext.at[9, 1:5, 0:4], local_sem.at[8]),
-        pltpu.make_async_copy(dist.at[7], ext.at[0, 1:5, 4:8], local_sem.at[9]),
-        pltpu.make_async_copy(level_hbm, level, local_sem.at[10]),
+        pltpu.make_async_copy(dist.at[8], ext.at[9, 1:5, 0:4], local_sem.at[2]),
+        pltpu.make_async_copy(dist.at[7], ext.at[0, 1:5, 4:8], local_sem.at[3]),
+        pltpu.make_async_copy(level_hbm, level, local_sem.at[4]),
     ]
     for load in loads:
         load.start()
@@ -121,14 +121,14 @@
         )
         return outer, middle
 
-    for load in loads[:4]:
+    for load in loads[:2]:
         load.wait()
     outer_y = jnp.where(even, 1, 4)
     for k, (first, width) in enumerate(SEGMENTS):
         y = 5 - outer_y if k == 2 else outer_y
         face[k, :, 0:width] = ext[1:9, y, :, first : first + width].reshape(64, width).astype(BF16)
 
-    for load in loads[4:]:
+    for load in loads[2:]:
         load.wait()
     edge = jnp.where(falling, ext[1, 1:5, 0:4], ext[8, 1:5, 4:8])
     edge_out[...] = edge.reshape(16, LOCAL).astype(BF16)
@@ -194,29 +194,38 @@
     first_z, last_z = z_at == 0, z_at == 3
     step_x = jnp.where(falling, 1, -1)
 
-    def rows(x, pair):
-        done = []
-        for rank in (2 * pair, 2 * pair + 1):
-            y = Y_ORDER[rank]
-            f = ext[x + 1, y + 1]
-            flux = a_x * (f - ext[x + 1 + step_x, y + 1])
-            flux = flux + a_y * (f - jnp.where(up_y, ext[x + 1, y], ext[x + 1, y + 2]))
-            low = jnp.where(first_z, pltpu.roll(f, 5, 0), pltpu.roll(f, 1, 0))
-            high = jnp.where(last_z, pltpu.roll(f, 3, 0), pltpu.roll(f, 7, 0))
-            flux = flux + a_z * (f - jnp.where(up_z, low, high))
-            read[x, rank] = f - flux
-            done.append(f - flux)
+    def keep(x, pair, done):
         at = pl.multiple_of(32 * x + 16 * pair, 16)
         values[pl.ds(at, 16), :] = jnp.concatenate(done, axis=0).astype(BF16)
 
+    def along_xz(x, y):
+        f = ext[x + 1, y + 1]
+        low = jnp.where(first_z, pltpu.roll(f, 5, 0), pltpu.roll(f, 1, 0))
+        high = jnp.where(last_z, pltpu.roll(f, 3, 0), pltpu.roll(f, 7, 0))
+        flux = a_x * (f - ext[x + 1 + step_x, y + 1])
+        return f - (flux + a_z * (f - jnp.where(up_z, low, high)))
+
+    def along_y(x, y):
+        return a_y * (ext[x + 1, y + 1] - jnp.where(up_y, ext[x + 1, y], ext[x + 1, y + 2]))
+
+    def before_halo(x):
+        done = []
+        for rank, y in enumerate(Y_ORDER):
+            left = along_xz(x, y)
+            if rank < 2:
+                left = left - along_y(x, y)
+                done.append(left)
+            read[x, rank] = left
+        keep(x, 0, done)
+
+    first_inner = jnp.where(falling, 0, 1)
+
+    def inner(k, _):
+        before_halo(first_inner + k)
+        return 0
+
     hear(0)
     tell(1)
-    first_inner = jnp.where(falling, 0, 1)
-
-    def inner(k, _):
-        rows(first_inner + k, 0)
-        return 0
-
     lax.fori_loop(0, 7, inner, 0)
     hear(1)
     tell(2)
@@ -243,13 +252,19 @@
     ext[9, 1:5, 4:8] = edge
     ext[0, 1:5, 0:4] = edge
 
-    rows(jnp.where(falling, 7, 0), 0)
+    before_halo(jnp.where(falling, 7, 0))
 
     def outer(x, _):
-        rows(x, 1)
+        done = []
+        for rank in (2, 3):
+            evolved = read[x, rank] - along_y(x, Y_ORDER[rank])
+            read[x, rank] = evolved
+            done.append(evolved)
+        keep(x, 1, done)
         return 0
 
     lax.fori_loop(0, 8, outer, 0)
+
     def by_place(ref, turn, device):
         return ref.at[turn, lax.rem(device, 2), device // 2]
 
@@ -276,7 +291,7 @@
         ).wait()
 
     for turn in range(TURNS):
-        chosen = dot(picker[64 * turn : 64 * turn + 64], values[...])
+        chosen = dot(picker[SLOTS * turn : SLOTS * (turn + 1)], values[...])
         send[turn] = chosen.reshape(GROUPS, CELLS, LOCAL).astype(BF16)
         if turn == 0:
             hear(2)
@@ -353,16 +368,21 @@
             by_place(back, turn, me), packed.at[turn, me], back_recv.at[turn]
         ).start()
 
-    for turn in range(TURNS):
+    def rates(first, last):
+        terms = [
+            packed[turn].astype(F32).reshape(SLOTS, LOCAL).astype(BF16) for turn in range(first, last)
+        ]
+        given = lax.dot_general(
+            placer[SLOTS * first : SLOTS * last], jnp.concatenate(terms, axis=0),
+            (((0,), (0,)), ((), ())), preferred_element_type=F32,
+        )
+        return given.reshape(8, 4, 8, LOCAL)
+
+    for turn in range(TURNS - 1):
         all_of(packed, turn, back_recv)
-        rates = lax.dot_general(
-            placer[64 * turn : 64 * turn + 64],
-            packed[turn].astype(F32).reshape(GROUPS * CELLS, LOCAL).astype(BF16),
-            (((0,), (0,)), ((), ())), preferred_element_type=F32,
-        )
-        evolved = read[...] + rates.reshape(8, 4, 8, LOCAL)
-        if turn < TURNS - 1:
-            read[...] = evolved
+    read[...] = read[...] + rates(0, TURNS - 1)
+    all_of(packed, TURNS - 1, back_recv)
+    evolved = read[...] + rates(TURNS - 1, TURNS)
     for part in range(2):
         for rank, y in enumerate(Y_ORDER):
             out[8 * part : 8 * part + 8, y] = evolved[:, rank, 4 * part : 4 * part + 4]
@@ -406,7 +426,7 @@
             pltpu.VMEM((3 * NV, PLANE), F32),
             pltpu.VMEM((3 * NV, FREQ), F32),
             pltpu.VMEM((4, 4, 16), jnp.int32),
-            dma((11,)), dma((7,)), pltpu.SemaphoreType.REGULAR((6,)), dma((3,)), dma((3,)),
+            dma((5,)), dma((7,)), pltpu.SemaphoreType.REGULAR((6,)), dma((3,)), dma((3,)),
             *[dma((TURNS,))] * 4,
         ],
         compiler_params=pltpu.CompilerParams(

time: 29.5 us -> 28.9 us (0.980)
  Pallas kernels: 28.5 us -> 27.9 us
    pallas_call x1, Pallas kernels: 28.5 us -> 27.9 us  [per_device(): pl.pallas_call(kernel, out_shape=pltpu.VMEM(distribution.shape, F32), in_...]
where the time goes in v6:
time: 28.9 us; the launch traced here: 28.8 us
  Pallas kernels  27.9 us (97%)
  local copies, waits for them, and re-layouts  0.93 us (3%)
    pallas_call x1, Pallas kernels, per_device(): pl.pallas_call(kernel, out_shape=pltpu.VMEM(distribution.shape, F32), in_...  27.9 us
    unnamed x1, local copies, waits for them, and re-layouts  0.93 us

profile of v6, /device:TPU:1, one launch (start us, length us, event | category | flops | bytes accessed | tf_op | source)
XLA Modules:
  0.0 28.8 jit_solution(616974404138968815)
XLA Ops:
  0.0 27.9 %shard_map.91 = f32[16,4,4,864]{3,2,1,0:T(4,128)S(1)} custom-call(f32[16,4,4,864]{3,2,1,0:T(4,128)} %dist.1, s32[4,4,16]{2,1,0:T(4,128)} %bitcast.7, f32[576,24]{1,0:T(8,128)} %bitcast.4, f32[576,24]{1,0:T(8,128)} %bitcast.5, f32[576,24]{1,0:T(8,128)} %bitcast.6, bf16[576,768]{1,0:T(8,128)(2,1)} %constant.8.clone.forward_hbm, ...), custom_call_target="tpu_custom_call" | custom-call | tf_op jit(solution)/shard_map/pallas_call | solution.py:404
  27.9 0.9 %copy.11 = f32[16,4,4,864]{3,2,1,0:T(4,128)} copy(f32[16,4,4,864]{3,2,1,0:T(4,128)S(1)} %shard_map.91) | data formatting | bytes 1769472

commit v7 on v6

--- a/solution.py
+++ b/solution.py
@@ -53,8 +53,8 @@
 
 
 def kernel(
-    dist, level_hbm, kernel_a, kernel_b, kernel_c, forward_hbm, inverse_hbm, into_hbm, from_hbm, out,
-    ext, face, halo, edge_out, edge_in, read, values, send, recv, back, packed, forward, inverse, into_x, from_x, raw, spread, sym, level,
+    dist, level_hbm, kernel_a, kernel_b, kernel_c, forward_hbm, inverse_hbm, into_hbm, from_hbm, read, packed, placer,
+    ext, face, halo, edge_out, edge_in, values, send, recv, back, forward, inverse, into_x, from_x, raw, spread, sym, level,
     local_sem, table_sem, hop_sem, face_send, face_recv, send_sem, recv_sem, back_send, back_recv,
 ):
     me = lax.axis_index("vel")
@@ -177,7 +177,7 @@
         (iota((128, 256), 0).astype(F32) == slot) & (jnp.broadcast_to(active, (128, 256)) > 0.5)
     ).astype(F32)
     picker = hot.astype(BF16)
-    placer = (hot * (0.25 * level_row)).astype(BF16)
+    placer[...] = (hot * (0.25 * level_row)).astype(BF16)
 
     lane = iota((1, LOCAL), 1) + me * LOCAL
 
@@ -373,7 +373,7 @@
             packed[turn].astype(F32).reshape(SLOTS, LOCAL).astype(BF16) for turn in range(first, last)
         ]
         given = lax.dot_general(
-            placer[SLOTS * first : SLOTS * last], jnp.concatenate(terms, axis=0),
+            placer[SLOTS * first : SLOTS * last, :], jnp.concatenate(terms, axis=0),
             (((0,), (0,)), ((), ())), preferred_element_type=F32,
         )
         return given.reshape(8, 4, 8, LOCAL)
@@ -382,13 +382,29 @@
         all_of(packed, turn, back_recv)
     read[...] = read[...] + rates(0, TURNS - 1)
     all_of(packed, TURNS - 1, back_recv)
-    evolved = read[...] + rates(TURNS - 1, TURNS)
-    for part in range(2):
-        for rank, y in enumerate(Y_ORDER):
-            out[8 * part : 8 * part + 8, y] = evolved[:, rank, 4 * part : 4 * part + 4]
     for turn in range(TURNS):
         others_of(send, turn, send_sem)
         others_of(packed, turn, back_send)
+
+
+def put_out(read, packed, placer, out, ready, sem):
+    terms = packed[TURNS - 1].astype(F32).reshape(SLOTS, LOCAL).astype(BF16)
+    given = lax.dot_general(
+        placer[SLOTS * (TURNS - 1) : SLOTS * TURNS, :], terms, (((0,), (0,)), ((), ())),
+        preferred_element_type=F32,
+    ).reshape(8, 4, 8, LOCAL)
+    copies = []
+    for k in range(4):
+        rows = slice(2 * k, 2 * k + 2)
+        evolved = read[rows] + given[rows]
+        for part in range(2):
+            here = slice(8 * part + 2 * k, 8 * part + 2 * k + 2)
+            for rank, y in enumerate(Y_ORDER):
+                ready[here, y] = evolved[:, rank, 4 * part : 4 * part + 4]
+            copies.append(pltpu.make_async_copy(ready.at[here], out.at[here], sem.at[2 * k + part]))
+            copies[-1].start()
+    for copy in copies:
+        copy.wait()
 
 
 def in_hbm(array):
@@ -401,23 +417,24 @@
     hbm = pl.BlockSpec(memory_space=pltpu.MemorySpace.HBM)
     vmem = pl.BlockSpec(memory_space=pltpu.VMEM)
     dma = pltpu.SemaphoreType.DMA
-    return pl.pallas_call(
+    whole = [
+        ((8, 4, 8, LOCAL), F32), ((TURNS, GROUPS, CELLS, LOCAL), BF16), ((TURNS * SLOTS, 256), BF16),
+    ]
+    parts = pl.pallas_call(
         kernel,
-        out_shape=pltpu.VMEM(distribution.shape, F32),
+        out_shape=[pltpu.VMEM(*one) for one in whole],
         in_specs=[hbm] * 9,
-        out_specs=vmem,
+        out_specs=[vmem] * 3,
         scratch_shapes=[
             pltpu.VMEM((10, 6, 8, LOCAL), F32),
             pltpu.VMEM((3, 64, SEG), BF16),
             pltpu.VMEM((3, 64, SEG), BF16),
             pltpu.VMEM((16, LOCAL), BF16),
             pltpu.VMEM((16, LOCAL), BF16),
-            pltpu.VMEM((8, 4, 8, LOCAL), F32),
             pltpu.VMEM((256, LOCAL), BF16),
             pltpu.VMEM((TURNS, GROUPS, CELLS, LOCAL), BF16),
             pltpu.VMEM((TURNS, 2, CHIPS, CELLS, LOCAL), BF16),
             pltpu.VMEM((TURNS, 2, CHIPS, CELLS, LOCAL), BF16),
-            pltpu.VMEM((TURNS, GROUPS, CELLS, LOCAL), BF16),
             pltpu.VMEM((PLANE, 2 * FREQ), BF16),
             pltpu.VMEM((2 * FREQ, PLANE), BF16),
             pltpu.VMEM((2 * ROWS, ROWS), BF16),
@@ -434,6 +451,15 @@
         ),
     )(*map(in_hbm, (distribution, refine_level.transpose(1, 2, 0), *kernels, *constants)))
 
+    return pl.pallas_call(
+        put_out,
+        out_shape=pltpu.HBM(distribution.shape, F32),
+        in_specs=[vmem] * 3,
+        out_specs=hbm,
+        scratch_shapes=[pltpu.VMEM(distribution.shape, F32), dma((8,))],
+        compiler_params=pltpu.CompilerParams(vmem_limit_bytes=16 << 20),
+    )(*(pltpu.with_memory_space_constraint(one, pltpu.MemorySpace.VMEM) for one in parts))
+
 
 def solution(mesh):
     in_specs = (P("cx", "cy", None, "vel"), P("cx", "cy", None), P(), P(), P())

time: 28.9 us -> 29 us (level)
  Pallas kernels: 27.9 us -> 28.9 us
  local copies, waits for them, and re-layouts: 0.93 us -> 0 us
    pallas_call x1 -> x2, Pallas kernels: 27.9 us -> 28.9 us  [the longest x1 27.6 us: per_device(): pl.pallas_call(kernel, out_shape=[pltpu.VMEM(*one) for one in whole], in_...]
    unnamed x1 -> x0, local copies, waits for them, and re-layouts: 0.93 us -> none
where the time goes in v7:
time: 29 us; the launch traced here: 28.9 us
  Pallas kernels  28.9 us (100%)
    pallas_call x1, Pallas kernels, per_device(): pl.pallas_call(kernel, out_shape=[pltpu.VMEM(*one) for one in whole], in_...  27.6 us
    pallas_call x1, Pallas kernels, per_device(): pl.pallas_call(put_out, out_shape=pltpu.HBM(distribution.shape, F32), in_...  1.27 us

profile of v7, /device:TPU:1, one launch (start us, length us, event | category | flops | bytes accessed | tf_op | source)
XLA Modules:
  0.0 28.9 jit_solution(6121693240044688737)
XLA Ops:
  0.0 27.6 %shard_map.91 = (f32[8,4,8,864]{3,2,1,0:T(8,128)S(1)}, bf16[4,16,2,864]{3,2,1,0:T(2,128)(2,1)S(1)}, bf16[128,256]{1,0:T(8,128)(2,1)S(1)}) custom-call(f32[16,4,4,864]{3,2,1,0:T(4,128)} %dist.1, s32[4,4,16]{2,1,0:T(4,128)} %bitcast.7, f32[576,24]{1,0:T(8,128)} %bitcast.4, f32[576,24]{1,0:T(8,128)} %bitcast.5, f32[576,24]{1,0:T(8,128)} %bitcast.6, ...), custom_call_target="tpu_custom_call" | custom-call | tf_op jit(solution)/shard_map/pallas_call | solution.py:423
  27.6 1.3 %shard_map.92 = f32[16,4,4,864]{3,2,1,0:T(4,128)} custom-call(f32[8,4,8,864]{3,2,1,0:T(8,128)S(1)} %get-tuple-element.8.read, bf16[4,16,2,864]{3,2,1,0:T(2,128)(2,1)S(1)} %get-tuple-element.9.packed, bf16[128,256]{1,0:T(8,128)(2,1)S(1)} %get-tuple-element.10.placer), custom_call_target="tpu_custom_call" | custom-call | tf_op jit(solution)/shard_map/pallas_call | solution.py:454
